TPU v7x, 128 devices: a whole 4x4x4 slice. The times are simulated.
128 devices in a mesh: grp: 16 (over z, y), cand: 8 (over x, core).
Axes of the slice: x: 4, y: 4, z: 4, core: 2. Of those that a mesh axis runs over, the one named last changes fastest.
Arguments:
- history: bfloat16 [128, 1024, 256], P(('grp', 'cand')), may hold values from -9 to 9
- lengths: int32 [128], P(('grp', 'cand')), may hold values from 128 to 1024
- target: bfloat16 [128, 64, 256], P('grp', 'cand'), may hold values from -6 to 6
- bag_ids: int32 [128, 64, 32, 4], P('grp', 'cand'), may hold values from 0 to 32767
- leaf_ids: int32 [128, 64, 64], P('grp', 'cand'), may hold values from 0 to 31
- table_piece: bfloat16 [128, 8192, 128], P(('grp', 'cand')), may hold values from -6 to 6
- leaf_table: bfloat16 [64, 32, 256], replicated, may hold values from -0.75 to 0.75
- w_query: bfloat16 [256, 128], replicated, may hold values from -0.375 to 0.375
- w_key: bfloat16 [256, 128], replicated, may hold values from -0.375 to 0.375
- w_pair: bfloat16 [256, 128], replicated, may hold values from -0.375 to 0.375
- a_out: bfloat16 [128], replicated, may hold values from -1 to 1
- w_first: bfloat16 [4864, 1024], replicated, may hold values from -0.078125 to 0.078125
- w_second: bfloat16 [1024, 512], replicated, may hold values from -0.25 to 0.25
- w_third: bfloat16 [512, 256], replicated, may hold values from -0.375 to 0.375
- w_out: bfloat16 [256], replicated, may hold values from -0.5 to 0.5
Outputs:
- logits: float32 [128, 64], P('grp', 'cand')
All inputs are finite; a program needn't handle non-finite values.
Results may differ from a plain program's by a relative error of at most 0.0092.
Values may be sent and summed in bfloat16 or wider, within the bound.
A program may use at most 128 MiB of HBM per device.

v0:
```python
import math

import jax
import jax.numpy as jnp
from jax import lax
from jax.sharding import PartitionSpec as P

SPLIT = 4


def interest_of(queries, history_rows, length, w_query, w_key, w_pair, a_out):
    n_items = queries.shape[0]
    block_size = math.gcd(n_items, 32)
    k_part = jnp.dot(history_rows, w_key, preferred_element_type=jnp.float32).T
    live_mask = jnp.arange(history_rows.shape[0], dtype=jnp.int32) < length
    pair_rows = w_pair.T.astype(jnp.float32)
    a_vector = a_out.astype(jnp.float32)

    def one_block(q_block):
        q_part = jnp.dot(q_block, w_query, preferred_element_type=jnp.float32)
        scaled = (q_block.astype(jnp.float32)[:, None, :] * pair_rows[None]).astype(jnp.bfloat16)
        raw_pair = lax.dot_general(
            scaled.reshape(-1, scaled.shape[2]),
            history_rows,
            (((1,), (1,)), ((), ())),
            preferred_element_type=jnp.float32,
        )
        raw_pair = raw_pair.reshape(q_block.shape[0], pair_rows.shape[0], history_rows.shape[0])
        unit_act = jax.nn.relu(raw_pair + q_part[:, :, None] + k_part[None])
        scores = jnp.einsum("bak,a->bk", unit_act, a_vector, precision=lax.Precision.HIGHEST)
        scores = jnp.where(live_mask[None], scores, 0.0).astype(jnp.bfloat16)
        return jnp.dot(scores, history_rows, preferred_element_type=jnp.float32)

    weighted = lax.map(
        one_block, queries.reshape(n_items // block_size, block_size, queries.shape[1])
    )
    inv_root = 1.0 / jnp.sqrt(length.astype(jnp.float32))
    return (weighted.reshape(n_items, -1) * inv_root).astype(jnp.bfloat16)


def leaf_embed(leaf_rows, leaf_table):
    tree_count, leaf_count, feat_width = leaf_table.shape
    one_hot = (leaf_rows[..., None] == jnp.arange(leaf_count, dtype=jnp.int32)).astype(jnp.bfloat16)
    one_hot = one_hot.reshape(leaf_rows.shape[0], tree_count * leaf_count)
    return jnp.dot(
        one_hot,
        leaf_table.reshape(tree_count * leaf_count, feat_width),
        preferred_element_type=jnp.float32,
    ).astype(jnp.bfloat16)


def pool_piece(offsets, rows_of):
    lookups, bag_size = offsets.shape
    piece_rows, emb_width = rows_of.shape
    block_cols = math.gcd(piece_rows, 1024)
    col_base = jnp.arange(block_cols, dtype=jnp.int32)

    def add_block(block_idx, total):
        start = (block_idx * block_cols).astype(jnp.int32)
        columns = col_base + start
        counts = jnp.zeros((lookups, block_cols), jnp.bfloat16)
        for bag_slot in range(bag_size):
            counts = counts + (offsets[:, bag_slot, None] == columns[None]).astype(jnp.bfloat16)
        block_rows = lax.dynamic_slice_in_dim(rows_of, start, block_cols, 0)
        return total + jnp.dot(counts, block_rows, preferred_element_type=jnp.float32)

    empty = jnp.zeros((lookups, emb_width), jnp.float32)
    return lax.fori_loop(0, piece_rows // block_cols, add_block, empty)


def on_device(
    history,
    lengths,
    target,
    bag_ids,
    leaf_ids,
    table_piece,
    leaf_table,
    w_query,
    w_key,
    w_pair,
    a_out,
    w_first,
    w_second,
    w_third,
    w_out,
):
    req_count, per_req, feat_width = target.shape
    local_rows = req_count * per_req
    history_all, lengths_all = (
        lax.all_gather(history, "cand", axis=0, tiled=True),
        lax.all_gather(lengths, "cand", axis=0, tiled=True),
    )

    def one_request(inputs):
        return interest_of(inputs[0], inputs[1], inputs[2], w_query, w_key, w_pair, a_out)

    interest = lax.map(one_request, (target, history_all, lengths_all))
    devices = lax.axis_size(("grp", "cand"))
    tables = devices // SPLIT
    bag_size = bag_ids.shape[3]
    emb_width = table_piece.shape[2]
    piece_rows = table_piece.shape[1]
    bag_rows = jnp.transpose(bag_ids.reshape(local_rows, tables, bag_size), (1, 2, 0))
    outgoing = jnp.repeat(bag_rows, SPLIT, axis=0)
    incoming = lax.all_to_all(outgoing, ("grp", "cand"), split_axis=0, concat_axis=0, tiled=True)
    quarter = lax.axis_index(("grp", "cand")) % SPLIT
    offsets = incoming - quarter * piece_rows
    flat_offsets = jnp.transpose(offsets, (0, 2, 1)).reshape(devices * local_rows, bag_size)
    running = pool_piece(flat_offsets, table_piece[0])
    partial_value = running.astype(jnp.bfloat16).reshape(devices, local_rows, emb_width)
    returned = lax.all_to_all(
        partial_value, ("grp", "cand"), split_axis=0, concat_axis=0, tiled=True
    )
    pooled = jnp.sum(
        returned.reshape(tables, SPLIT, local_rows, emb_width), axis=1, dtype=jnp.float32
    ).astype(jnp.bfloat16)
    leaf_vec = leaf_embed(leaf_ids.reshape(local_rows, -1), leaf_table)
    table_width = tables * emb_width
    hidden_one = jnp.einsum(
        "tne,teh->nh",
        pooled,
        w_first[:table_width].reshape(tables, emb_width, -1),
        preferred_element_type=jnp.float32,
    )
    tail_feats = jnp.concatenate(
        [
            interest.reshape(local_rows, feat_width),
            target.reshape(local_rows, feat_width),
            leaf_vec,
        ],
        axis=1,
    )
    hidden_one = hidden_one + jnp.dot(
        tail_feats, w_first[table_width:], preferred_element_type=jnp.float32
    )
    hidden_one = jax.nn.relu(hidden_one).astype(jnp.bfloat16)
    hidden_two = jax.nn.relu(
        jnp.dot(hidden_one, w_second, preferred_element_type=jnp.float32)
    ).astype(jnp.bfloat16)
    hidden_three = jax.nn.relu(
        jnp.dot(hidden_two, w_third, preferred_element_type=jnp.float32)
    ).astype(jnp.bfloat16)
    logits = jnp.dot(hidden_three, w_out, preferred_element_type=jnp.float32)
    return logits.reshape(req_count, per_req)


def solution(mesh):
    placed = (
        P(("grp", "cand"), None, None),
        P(("grp", "cand")),
        P("grp", "cand", None),
        P("grp", "cand", None, None),
        P("grp", "cand", None),
        P(("grp", "cand"), None, None),
        P(),
        P(),
        P(),
        P(),
        P(),
        P(),
        P(),
        P(),
        P(),
    )
    return jax.shard_map(
        on_device, mesh=mesh, in_specs=placed, out_specs=P("grp", "cand"), check_vma=False
    )
```

profile of v0, /device:TPU:1, one launch (start us, length us, event | category | flops | bytes accessed | tf_op | source)
XLA Modules:
  0.0 293.0 jit_solution(519989076731727640)
XLA Ops:
  6.5 1.1 copy.21
  7.7 0.9 reshape.81
  8.6 11.5 %all-to-all-start = ((s32[128,1,256]{2,1,0:T(1,128)}), s32[128,1,256]{2,1,0:T(1,128)S(1)}, u32[]{:S(2)}, u32[]{:S(2)}) async-start(s32[128,1,256]{2,1,0:T(1,128)} %reshape.81), calls=%async_computation | async-start | bytes 262144 | tf_op jit(solution)/shard_map/all_to_all | solution.py:106
  20.1 0.7 all-gather.2.cloned.1.call-update
  20.8 9.2 %all-to-all-done = s32[128,1,256]{2,1,0:T(1,128)S(1)} async-done(((s32[128,1,256]{2,1,0:T(1,128)}), s32[128,1,256]{2,1,0:T(1,128)S(1)}, u32[]{:S(2)}, u32[]{:S(2)}) %all-to-all-start) | async-done | bytes 131104 | tf_op jit(solution)/shard_map/all_to_all | solution.py:106
  30.7 1.0 reduce.1
  32.1 132.7 %while.29 = (s32[]{:T(128)}, f32[8192,128]{1,0:T(8,128)}, s32[8192,4]{0,1:T(4,128)S(1)}, bf16[8192,128]{1,0:T(8,128)(2,1)}, s32[]{:T(128)}, /*index=5*/s32[]{:T(128)}, s32[]{:T(128)}, s32[]{:T(128)}) while((s32[]{:T(128)}, f32[8192,128]{1,0:T(8,128)}, s32[8192,4]{0,1:T(4,128)S(1)}, bf16[8192,128]{1,0:T(8,128)(2,1)}, s32[]{:T(128)}, ...), condition=%wide.region_1.2_spmd.clone, body=%wide.region_0.1_spmd.clone.sunk | while | flops 2241856512 | bytes 9052317 | solution.py:68
  32.2 16.4 %fusion.133 = f32[8192,128]{1,0:T(8,128)} fusion(s32[1024]{0:T(1024)S(1)} %iota_add_fusion.2, s32[8192]{0:T(1024)S(1)} %bitcast.104, s32[8192]{0:T(1024)S(1)} %bitcast.105, s32[8192]{0:T(1024)S(1)} %bitcast.106, s32[8192]{0:T(1024)S(1)} %bitcast.103, f32[8192,128]{1,0:T(8,128)} %get-tuple-element.328, pred[]{:T(512)S(6)} %compare.4, ...), kind=kOutput, calls=%fused_computation.52.clone.1 | convolution fusion | flops 2241855488 | bytes 8785925 | tf_op jit(solution)/shard_map/while/body/eval_jaxpr/dot_general | solution.py:65
  48.7 16.5 %fusion.133 = f32[8192,128]{1,0:T(8,128)} fusion(s32[1024]{0:T(1024)S(1)} %iota_add_fusion.2, s32[8192]{0:T(1024)S(1)} %bitcast.104, s32[8192]{0:T(1024)S(1)} %bitcast.105, s32[8192]{0:T(1024)S(1)} %bitcast.106, s32[8192]{0:T(1024)S(1)} %bitcast.103, f32[8192,128]{1,0:T(8,128)} %get-tuple-element.328, pred[]{:T(512)S(6)} %compare.4, ...), kind=kOutput, calls=%fused_computation.52.clone.1 | convolution fusion | flops 2241855488 | bytes 8785925 | tf_op jit(solution)/shard_map/while/body/eval_jaxpr/dot_general | solution.py:65
  65.3 16.5 %fusion.133 = f32[8192,128]{1,0:T(8,128)} fusion(s32[1024]{0:T(1024)S(1)} %iota_add_fusion.2, s32[8192]{0:T(1024)S(1)} %bitcast.104, s32[8192]{0:T(1024)S(1)} %bitcast.105, s32[8192]{0:T(1024)S(1)} %bitcast.106, s32[8192]{0:T(1024)S(1)} %bitcast.103, f32[8192,128]{1,0:T(8,128)} %get-tuple-element.328, pred[]{:T(512)S(6)} %compare.4, ...), kind=kOutput, calls=%fused_computation.52.clone.1 | convolution fusion | flops 2241855488 | bytes 8785925 | tf_op jit(solution)/shard_map/while/body/eval_jaxpr/dot_general | solution.py:65
  81.9 16.5 %fusion.133 = f32[8192,128]{1,0:T(8,128)} fusion(s32[1024]{0:T(1024)S(1)} %iota_add_fusion.2, s32[8192]{0:T(1024)S(1)} %bitcast.104, s32[8192]{0:T(1024)S(1)} %bitcast.105, s32[8192]{0:T(1024)S(1)} %bitcast.106, s32[8192]{0:T(1024)S(1)} %bitcast.103, f32[8192,128]{1,0:T(8,128)} %get-tuple-element.328, pred[]{:T(512)S(6)} %compare.4, ...), kind=kOutput, calls=%fused_computation.52.clone.1 | convolution fusion | flops 2241855488 | bytes 8785925 | tf_op jit(solution)/shard_map/while/body/eval_jaxpr/dot_general | solution.py:65
  98.5 16.5 %fusion.133 = f32[8192,128]{1,0:T(8,128)} fusion(s32[1024]{0:T(1024)S(1)} %iota_add_fusion.2, s32[8192]{0:T(1024)S(1)} %bitcast.104, s32[8192]{0:T(1024)S(1)} %bitcast.105, s32[8192]{0:T(1024)S(1)} %bitcast.106, s32[8192]{0:T(1024)S(1)} %bitcast.103, f32[8192,128]{1,0:T(8,128)} %get-tuple-element.328, pred[]{:T(512)S(6)} %compare.4, ...), kind=kOutput, calls=%fused_computation.52.clone.1 | convolution fusion | flops 2241855488 | bytes 8785925 | tf_op jit(solution)/shard_map/while/body/eval_jaxpr/dot_general | solution.py:65
  115.1 16.5 %fusion.133 = f32[8192,128]{1,0:T(8,128)} fusion(s32[1024]{0:T(1024)S(1)} %iota_add_fusion.2, s32[8192]{0:T(1024)S(1)} %bitcast.104, s32[8192]{0:T(1024)S(1)} %bitcast.105, s32[8192]{0:T(1024)S(1)} %bitcast.106, s32[8192]{0:T(1024)S(1)} %bitcast.103, f32[8192,128]{1,0:T(8,128)} %get-tuple-element.328, pred[]{:T(512)S(6)} %compare.4, ...), kind=kOutput, calls=%fused_computation.52.clone.1 | convolution fusion | flops 2241855488 | bytes 8785925 | tf_op jit(solution)/shard_map/while/body/eval_jaxpr/dot_general | solution.py:65
  131.7 16.5 %fusion.133 = f32[8192,128]{1,0:T(8,128)} fusion(s32[1024]{0:T(1024)S(1)} %iota_add_fusion.2, s32[8192]{0:T(1024)S(1)} %bitcast.104, s32[8192]{0:T(1024)S(1)} %bitcast.105, s32[8192]{0:T(1024)S(1)} %bitcast.106, s32[8192]{0:T(1024)S(1)} %bitcast.103, f32[8192,128]{1,0:T(8,128)} %get-tuple-element.328, pred[]{:T(512)S(6)} %compare.4, ...), kind=kOutput, calls=%fused_computation.52.clone.1 | convolution fusion | flops 2241855488 | bytes 8785925 | tf_op jit(solution)/shard_map/while/body/eval_jaxpr/dot_general | solution.py:65
  148.3 16.5 %fusion.133 = f32[8192,128]{1,0:T(8,128)} fusion(s32[1024]{0:T(1024)S(1)} %iota_add_fusion.2, s32[8192]{0:T(1024)S(1)} %bitcast.104, s32[8192]{0:T(1024)S(1)} %bitcast.105, s32[8192]{0:T(1024)S(1)} %bitcast.106, s32[8192]{0:T(1024)S(1)} %bitcast.103, f32[8192,128]{1,0:T(8,128)} %get-tuple-element.328, pred[]{:T(512)S(6)} %compare.4, ...), kind=kOutput, calls=%fused_computation.52.clone.1 | convolution fusion | flops 2241855488 | bytes 8785925 | tf_op jit(solution)/shard_map/while/body/eval_jaxpr/dot_general | solution.py:65
  164.8 3.8 %convert_element_type.81 = bf16[8192,128]{1,0:T(8,128)(2,1)} convert(f32[8192,128]{1,0:T(8,128)} %get-tuple-element.173) | non-fusion elementwise | flops 1048576 | bytes 6291456 | tf_op jit(solution)/shard_map/convert_element_type | solution.py:111
  168.6 4.2 %all-to-all-start.1 = ((bf16[128,64,128]{2,1,0:T(8,128)(2,1)}), bf16[128,64,128]{2,1,0:T(8,128)(2,1)S(1)}, u32[]{:S(2)}, u32[]{:S(2)}) async-start(bf16[128,64,128]{2,1,0:T(8,128)(2,1)} %bitcast.14), calls=%async_computation.1 | async-start | bytes 4194304 | tf_op jit(solution)/shard_map/all_to_all | solution.py:112
  174.1 0.7 dynamic-update-slice
  174.8 25.6 %all-reduce = s32[8]{0:T(128)S(1)} all-reduce(s32[8]{0:T(128)S(1)} %dynamic-update-slice), channel_id=1, replica_groups=mesh['grp'=16,'cand'=8] {'cand'}, use_global_device_ids=true, to_apply=%add | all-reduce | flops 8 | bytes 64
  200.7 7.7 %slice.34 = bf16[4096,1024]{1,0:T(8,128)(2,1)} slice(bf16[4864,1024]{1,0:T(8,128)(2,1)} %param.30), slice={[0:4096], [0:1024]} | slice | bytes 16777216 | tf_op jit(solution)/shard_map/slice | solution.py:123
  209.2 5.0 %convolution_bitcast_fusion.1 = f32[64,1024]{1,0:T(8,128)S(1)} fusion(bf16[32,64,128]{2,1,0:T(8,128)(2,1)S(1)} %bitcast_reduce_fusion, bf16[32,128,1024]{2,1,0:T(8,128)(2,1)} %bitcast.101), kind=kOutput, calls=%fused_computation.60 | convolution fusion | flops 536870912 | bytes 9175040 | tf_op jit(solution)/shard_map/tne,teh->nh/dot_general | solution.py:120
  214.4 68.9 %while.28 = (s32[]{:T(128)}, bf16[8,8,256]{2,1,0:T(8,128)(2,1)S(1)}, s32[8]{0:T(128)S(1)}, bf16[8,8,256]{2,1,0:T(8,128)(2,1)S(1)}, bf16[256,128]{0,1:T(8,128)(2,...) while((s32[]{:T(128)}, ...), condition=%wide.region_4.5_spmd, body=%wide.region_3.4_spmd.sunk | while | flops 624999424 | bytes 12607389 | solution.py:98
  215.7 0.6 iota_compare_fusion.4
  216.5 1.3 convolution_bitcast_fusion.4
  218.0 1.8 fusion.126
  219.8 1.9 fusion.128
  221.7 1.2 fusion.129
  224.3 0.6 iota_compare_fusion.4
  225.1 1.3 convolution_bitcast_fusion.4
  226.6 1.8 fusion.126
  228.4 1.9 fusion.128
  230.3 1.2 fusion.129
  232.9 0.6 iota_compare_fusion.4
  233.7 1.3 convolution_bitcast_fusion.4
  235.2 1.8 fusion.126
  237.0 1.9 fusion.128
  239.0 1.2 fusion.129
  241.5 0.6 iota_compare_fusion.4
  242.3 1.3 convolution_bitcast_fusion.4
  243.8 1.8 fusion.126
  245.6 1.9 fusion.128
  247.6 1.2 fusion.129
  250.1 0.6 iota_compare_fusion.4
  250.9 1.3 convolution_bitcast_fusion.4
  252.4 1.8 fusion.126
  254.2 1.9 fusion.128
  256.2 1.2 fusion.129
  258.7 0.6 iota_compare_fusion.4
  259.5 1.3 convolution_bitcast_fusion.4
  261.0 1.8 fusion.126
  262.8 1.9 fusion.128
  264.8 1.2 fusion.129
  267.3 0.6 iota_compare_fusion.4
  268.1 1.3 convolution_bitcast_fusion.4
  269.6 1.8 fusion.126
  271.4 1.9 fusion.128
  273.4 1.2 fusion.129
  275.9 0.6 iota_compare_fusion.4
  276.7 1.3 convolution_bitcast_fusion.4
  278.2 1.8 fusion.126
  280.0 1.9 fusion.128
  282.0 1.2 fusion.129
  283.2 2.0 fusion.66
  285.5 0.7 reshape.68
  (97 shorter events, 11.5 us)
Async XLA Ops:
  6.5 276.7 %copy-start = (bf16[1024,512]{1,0:T(8,128)(2,1)S(1)}, bf16[1024,512]{1,0:T(8,128)(2,1)}, u32[]{:S(2)}) copy-start(bf16[1024,512]{1,0:T(8,128)(2,1)} %param.31) | copy-start | bytes 3145732
  8.6 21.5 %all-to-all-start = ((s32[128,1,256]{2,1,0:T(1,128)}), s32[128,1,256]{2,1,0:T(1,128)S(1)}, u32[]{:S(2)}, u32[]{:S(2)}) async-start(s32[128,1,256]{2,1,0:T(1,128)} %reshape.81), calls=%async_computation | async-start | bytes 262144 | tf_op jit(solution)/shard_map/all_to_all | solution.py:106
  20.1 194.2 %all-gather.2.cloned.1.call-start = ((), (), s32[]{:S(2)}) async-start(), calls=%async_computation.2 | async-start | bytes 4718592 | tf_op jit(solution)/shard_map/all_gather | solution.py:91
  164.8 8.7 %copy-start.10 = (u32[128]{0:T(128)S(1)}, u32[128]{0:T(128)}, u32[]{:S(2)}) copy-start(u32[128]{0:T(128)} %constant.102) | copy-start | bytes 1540
  164.8 35.6 %copy-start.9 = (bf16[256]{0:T(256)(128)(2,1)S(1)}, bf16[256]{0:T(256)(128)(2,1)}, u32[]{:S(2)}) copy-start(bf16[256]{0:T(256)(128)(2,1)} %param.33) | copy-start | bytes 1540
  164.8 35.6 %copy-start.7 = (s32[8,8,64]{2,1,0:T(8,128)S(1)}, s32[8,8,64]{2,1,0:T(8,128)}, u32[]{:S(2)}) copy-start(s32[8,8,64]{2,1,0:T(8,128)} %param.23) | copy-start | bytes 49156
  164.8 35.7 %copy-start.6 = (bf16[256,128]{1,0:T(8,128)(2,1)S(1)}, bf16[256,128]{1,0:T(8,128)(2,1)}, u32[]{:S(2)}) copy-start(bf16[256,128]{1,0:T(8,128)(2,1)} %param.28) | copy-start | bytes 196612
  168.6 40.2 %all-to-all-start.1 = ((bf16[128,64,128]{2,1,0:T(8,128)(2,1)}), bf16[128,64,128]{2,1,0:T(8,128)(2,1)S(1)}, u32[]{:S(2)}, u32[]{:S(2)}) async-start(bf16[128,64,128]{2,1,0:T(8,128)(2,1)} %bitcast.14), calls=%async_computation.1 | async-start | bytes 4194304 | tf_op jit(solution)/shard_map/all_to_all | solution.py:112
  200.6 7.7 %copy-start.3 = (bf16[64,32,256]{2,1,0:T(8,128)(2,1)S(1)}, bf16[64,32,256]{2,1,0:T(8,128)(2,1)}, u32[]{:S(2)}) copy-start(bf16[64,32,256]{2,1,0:T(8,128)(2,1)} %param.25) | copy-start | bytes 3145732
  209.2 5.1 %copy-start.1 = (bf16[256,128]{1,0:T(8,128)(2,1)S(1)}, bf16[256,128]{1,0:T(8,128)(2,1)}, u32[]{:S(2)}) copy-start(bf16[256,128]{1,0:T(8,128)(2,1)} %param.27) | copy-start | bytes 196612
  209.2 5.1 %copy-start.2 = (bf16[256,128]{1,0:T(8,128)(2,1)S(1)}, bf16[256,128]{1,0:T(8,128)(2,1)}, u32[]{:S(2)}) copy-start(bf16[256,128]{1,0:T(8,128)(2,1)} %param.26) | copy-start | bytes 196612
  209.2 5.1 %copy-start.5 = (bf16[8,8,256]{2,1,0:T(8,128)(2,1)S(1)}, bf16[8,8,256]{2,1,0:T(8,128)(2,1)}, u32[]{:S(2)}) copy-start(bf16[8,8,256]{2,1,0:T(8,128)(2,1)} %param.21) | copy-start | bytes 98308
  209.2 5.1 %copy-start.8 = (bf16[128]{0:T(256)(128)(2,1)S(1)}, bf16[128]{0:T(256)(128)(2,1)}, u32[]{:S(2)}) copy-start(bf16[128]{0:T(256)(128)(2,1)} %param.29) | copy-start | bytes 772
  214.3 70.9 %copy-start.4 = (bf16[512,256]{1,0:T(8,128)(2,1)S(1)}, bf16[512,256]{1,0:T(8,128)(2,1)}, u32[]{:S(2)}) copy-start(bf16[512,256]{1,0:T(8,128)(2,1)} %param.32) | copy-start | bytes 786436
Sparse Core Ops, SparseCore 0:
  22.6 33.8 all-gather.1
where the time goes:
time: 295 us; the launch traced here: 293 us
  matrix products  191 us (65%)
  blocking collectives  25.6 us (9%)
  local copies, waits for them, and re-layouts  20.1 us (7%)
  starting transfers between devices  15.7 us (5%)
  between operations  14.3 us (5%)
  other arithmetic  10.4 us (4%)
  waiting for transfers between devices  9.95 us (3%)
  loops' own time  5.82 us (2%)
    dot_general x8, matrix products, add_block(): jnp.dot(counts, block_rows, preferred_element_type=jnp.float32)  132 us
    unnamed x1, blocking collectives  25.6 us
    dot_general x8, matrix products, one_block(): jnp.einsum('bak,a->bk', unit_act, a_vector, precision=lax.Precision.HIGHEST)  15.5 us
    dot_general x8, matrix products, one_block(): lax.dot_general(scaled.reshape(-1, scaled.shape[2]), history_rows, (((1,)...  14.3 us
    all_to_all x1, starting transfers between devices, on_device(): lax.all_to_all(outgoing, ('grp', 'cand'), split_axis=0, concat_axis=0, ti...  11.5 us
    dot_general x8, matrix products, interest_of(): k_part = jnp.dot(history_rows, w_key, preferred_element_type=jnp.float32).T  10.7 us
    dot_general x8, matrix products, one_block(): return jnp.dot(scores, history_rows, preferred_element_type=jnp.float32)  9.8 us
    all_to_all x1, waiting for transfers between devices, on_device(): lax.all_to_all(outgoing, ('grp', 'cand'), split_axis=0, concat_axis=0, ti...  9.24 us
  transfers between devices with their start and end apart: 3, of which 1 were waited for; matrix products, arithmetic and copies ran while one was open for 52% of the time, Pallas kernels for 0%

commit v1 on v0

v1 whole, which is shorter than its diff:
```python
import functools

import jax
import jax.numpy as jnp
from jax import lax
from jax.experimental import pallas as pl
from jax.experimental.pallas import tpu as pltpu
from jax.sharding import PartitionSpec as P

MESH = pl.DeviceIdType.MESH
SPLIT = 4
F32 = jnp.float32
BF16 = jnp.bfloat16


class Place:
    def __init__(self, n_grp, n_cand):
        self.n_cand = n_cand
        self.chips_x = n_cand // 2
        self.chips = n_grp * self.chips_x
        self.grp = lax.axis_index("grp")
        self.cand = lax.axis_index("cand")
        self.core = lax.rem(self.cand, 2)
        self.x = lax.div(self.cand, 2)
        self.chip = self.grp * self.chips_x + self.x

    def same_core(self, chip):
        return (lax.div(chip, self.chips_x), 2 * lax.rem(chip, self.chips_x) + self.core)

    def other_core(self, step):
        return (self.grp, 2 * lax.rem(self.x + step, self.chips_x) + 1 - self.core)

    def chip_after(self, step):
        return lax.rem(self.chip + step, self.chips)

    def enter(self):
        barrier = pltpu.get_barrier_semaphore()

        def greet_same(step, carry):
            pl.semaphore_signal(
                barrier, inc=1, device_id=self.same_core(self.chip_after(step)), device_id_type=MESH
            )
            return carry

        lax.fori_loop(1, self.chips, greet_same, 0)
        for step in range(self.chips_x):
            pl.semaphore_signal(barrier, inc=1, device_id=self.other_core(step), device_id_type=MESH)
        return barrier, self.chips - 1 + self.chips_x


def exchange_kernel(
    n_grp, n_cand, ids_ref, target_ref, piece_ref, ids_out, target_out, piece_out,
    ids_send, ids_recv, t_send, t_recv, swap_send, swap_recv, own_sem,
):
    at = Place(n_grp, n_cand)
    barrier, count = at.enter()
    own_ids = pltpu.make_async_copy(ids_ref.at[at.chip], ids_out.at[at.chip], own_sem.at[0])
    own_target = pltpu.make_async_copy(target_ref.at[at.cand], target_out.at[at.cand], own_sem.at[1])
    own_ids.start()
    own_target.start()
    pl.semaphore_wait(barrier, count)

    def send_ids(step):
        to = at.chip_after(step)
        return pltpu.make_async_remote_copy(
            src_ref=ids_ref.at[to], dst_ref=ids_out.at[at.chip],
            send_sem=ids_send.at[step], recv_sem=ids_recv.at[at.chip],
            device_id=at.same_core(to), device_id_type=MESH,
        )

    def from_chip(step):
        chip = at.chip_after(step)
        return pltpu.make_async_remote_copy(
            src_ref=ids_ref.at[chip], dst_ref=ids_out.at[chip],
            send_sem=ids_send.at[step], recv_sem=ids_recv.at[chip],
            device_id=at.same_core(chip), device_id_type=MESH,
        )

    def send_target(step):
        to = lax.rem(at.cand + step, n_cand)
        return pltpu.make_async_remote_copy(
            src_ref=target_ref.at[to], dst_ref=target_out.at[at.cand],
            send_sem=t_send.at[step], recv_sem=t_recv.at[at.cand],
            device_id=(at.grp, to), device_id_type=MESH,
        )

    def target_from(step):
        cand = lax.rem(at.cand + step, n_cand)
        return pltpu.make_async_remote_copy(
            src_ref=target_ref.at[cand], dst_ref=target_out.at[cand],
            send_sem=t_send.at[step], recv_sem=t_recv.at[cand],
            device_id=(at.grp, cand), device_id_type=MESH,
        )

    def loop(first, last, act):
        def body(step, carry):
            act(step)
            return carry

        lax.fori_loop(first, last, body, 0)

    swap = pltpu.make_async_remote_copy(
        src_ref=piece_ref.at[0], dst_ref=piece_out, send_sem=swap_send, recv_sem=swap_recv,
        device_id=at.other_core(0), device_id_type=MESH,
    )
    loop(1, at.chips, lambda step: send_ids(step).start())
    loop(1, n_cand, lambda step: send_target(step).start())
    swap.start()
    own_ids.wait()
    own_target.wait()
    loop(1, n_cand, lambda step: target_from(step).wait_recv())
    loop(1, at.chips, lambda step: from_chip(step).wait_recv())
    loop(1, n_cand, lambda step: send_target(step).wait_send())
    loop(1, at.chips, lambda step: send_ids(step).wait_send())
    swap.wait()


def pool_kernel(bag, per_src, ids_ref, own_ref, other_ref, out_ref, table, total):
    piece_rows = other_ref.shape[0]
    core = lax.rem(lax.axis_index("cand"), 2)
    half = 512

    def widen(i, carry):
        at = pl.multiple_of(i * half, half)
        mine = pl.multiple_of(core * piece_rows + i * half, half)
        theirs = pl.multiple_of((1 - core) * piece_rows + i * half, half)
        table[pl.ds(mine, half), :] = own_ref[0, pl.ds(at, half), :].astype(F32)
        table[pl.ds(theirs, half), :] = other_ref[pl.ds(at, half), :].astype(F32)
        return carry

    lax.fori_loop(0, piece_rows // half, widen, 0)
    table[pl.ds(2 * piece_rows, 8), :] = jnp.zeros((8, table.shape[1]), F32)

    def one_source(src, carry):
        for row in range(per_src):
            total_row = None
            for slot in range(bag):
                at = ids_ref[src, row * bag + slot]
                got = table[pl.ds(at, 1), :]
                total_row = got if total_row is None else total_row + got
            total[pl.ds(src * per_src + row, 1), :] = total_row
        return carry

    lax.fori_loop(0, ids_ref.shape[0], one_source, 0)

    def narrow(src, carry):
        at = pl.multiple_of(src * per_src, per_src)
        out_ref[src] = total[pl.ds(at, per_src), :].astype(BF16)
        return carry

    lax.fori_loop(0, out_ref.shape[0], narrow, 0)


def score_kernel(
    n_grp, n_cand, sums_ref, length_ref, cands_ref, target_ref, leaf_ids_ref, history_hbm,
    leaf_hbm, w_query_ref, w_key_ref, w_pair_ref, a_out_ref, w_first_hbm, w_second_hbm, w_third_hbm,
    w_out_ref, out_ref,
    got, back, interest, history, leaf_table, w_first, w_second, w_third, scores, comb, pooled,
    sum_send, sum_recv, back_send, back_recv, load_sem,
):
    at = Place(n_grp, n_cand)
    barrier, count = at.enter()
    loads = [
        pltpu.make_async_copy(src, dst, load_sem.at[i])
        for i, (src, dst) in enumerate(
            [
                (history_hbm.at[0], history),
                (leaf_hbm, leaf_table),
                (w_first_hbm, w_first),
                (w_second_hbm, w_second),
                (w_third_hbm, w_third),
                (sums_ref.at[at.chip], got.at[at.chip]),
            ]
        )
    ]
    for load in loads:
        load.start()

    def loop(first, last, act):
        def body(step, carry):
            act(step)
            return carry

        lax.fori_loop(first, last, body, 0)

    def send_sums(step):
        to = at.chip_after(step)
        return pltpu.make_async_remote_copy(
            src_ref=sums_ref.at[to], dst_ref=got.at[at.chip],
            send_sem=sum_send.at[step], recv_sem=sum_recv.at[at.chip],
            device_id=at.same_core(to), device_id_type=MESH,
        )

    def sums_from(step):
        chip = at.chip_after(step)
        return pltpu.make_async_remote_copy(
            src_ref=sums_ref.at[chip], dst_ref=got.at[chip],
            send_sem=sum_send.at[step], recv_sem=sum_recv.at[chip],
            device_id=at.same_core(chip), device_id_type=MESH,
        )

    def send_back(step):
        to = lax.rem(at.cand + step, n_cand)
        return pltpu.make_async_remote_copy(
            src_ref=interest.at[to], dst_ref=back.at[at.cand],
            send_sem=back_send.at[step], recv_sem=back_recv.at[at.cand],
            device_id=(at.grp, to), device_id_type=MESH,
        )

    def back_from(step):
        cand = lax.rem(at.cand + step, n_cand)
        return pltpu.make_async_remote_copy(
            src_ref=interest.at[cand], dst_ref=back.at[cand],
            send_sem=back_send.at[step], recv_sem=back_recv.at[cand],
            device_id=(at.grp, cand), device_id_type=MESH,
        )

    pl.semaphore_wait(barrier, count)
    loop(1, at.chips, lambda step: send_sums(step).start())

    loads[0].wait()
    events, width = history.shape
    att = w_pair_ref.shape[1]
    per_src = cands_ref.shape[1]
    pair_t = w_pair_ref[...].astype(F32).T
    key_t = w_key_ref[...].astype(F32).T
    query_t = w_query_ref[...].astype(F32).T.astype(BF16)
    a_col = a_out_ref[...].astype(F32).T
    a_wide = jnp.broadcast_to(a_col, (att, 256))
    history_t = history[...].astype(F32).T.astype(BF16)
    length = length_ref[0]
    column = lax.broadcasted_iota(jnp.int32, (per_src, events), 1)

    def one_group(g, carry):
        rows = cands_ref[g]
        rows_f = rows.astype(F32)
        q_part = lax.dot_general(query_t, rows, (((1,), (1,)), ((), ())), preferred_element_type=F32)
        base = jnp.sum(q_part * a_col, axis=0, keepdims=True)
        for c in range(per_src):
            comb[pl.ds(c * att, att), :] = (rows_f[c : c + 1, :] * pair_t + key_t).astype(BF16)
        for block in range(events // 256):
            cols = pl.ds(block * 256, 256)
            raw = jnp.dot(comb[...], history_t[:, block * 256 : block * 256 + 256], preferred_element_type=F32)
            for c in range(per_src):
                unit = jnp.maximum(raw[c * att : (c + 1) * att, :], -q_part[:, c : c + 1]) * a_wide
                line = jnp.sum(unit, axis=0, keepdims=True) + base[:, c : c + 1]
                scores[pl.ds(g * per_src + c, 1), cols] = line
        return carry

    lax.fori_loop(0, n_cand, one_group, 0)
    live = lax.broadcasted_iota(jnp.int32, scores.shape, 1) < length
    weights = jnp.where(live, scores[...], 0.0).astype(BF16)
    weighted = jnp.dot(weights, history[...], preferred_element_type=F32)
    root = jnp.sqrt(jnp.full((1, 1), length, jnp.int32).astype(F32))
    weighted = weighted * (1.0 / root)
    interest[...] = weighted.reshape(interest.shape)

    loads[1].wait()
    n_rows, trees = leaf_ids_ref.shape
    leaves = leaf_table.shape[0] // trees
    spread_row = lax.broadcasted_iota(jnp.int32, (trees, trees * leaves), 0)
    spread_col = lax.broadcasted_iota(jnp.int32, (trees, trees * leaves), 1)
    spread = (spread_row == spread_col // leaves).astype(F32).astype(BF16)
    ids = leaf_ids_ref[...].astype(F32).astype(BF16)
    wide = jnp.dot(ids, spread, preferred_element_type=F32)
    leaf_of = lax.broadcasted_iota(jnp.int32, wide.shape, 1) % leaves
    hot = (wide == leaf_of.astype(F32)).astype(F32).astype(BF16)
    leaf_vec = jnp.dot(hot, leaf_table[...], preferred_element_type=F32).astype(BF16)

    loop(1, n_cand, lambda step: send_back(step).start())
    back[at.cand] = interest[at.cand]

    loads[2].wait()
    table_width = w_first.shape[0] - 3 * width
    hidden = jnp.dot(
        target_ref[...], w_first[pl.ds(table_width + width, width), :], preferred_element_type=F32
    )
    hidden += jnp.dot(leaf_vec, w_first[pl.ds(table_width + 2 * width, width), :], preferred_element_type=F32)

    loads[3].wait()
    loads[4].wait()
    loads[5].wait()
    loop(1, n_cand, lambda step: back_from(step).wait_recv())
    seen = back[...].reshape(n_rows, width).astype(BF16)
    hidden += jnp.dot(seen, w_first[pl.ds(table_width, width), :], preferred_element_type=F32)
    loop(1, at.chips, lambda step: sums_from(step).wait_recv())
    emb = got.shape[2]
    for t in range(got.shape[0] // 2):
        pooled[:, pl.ds(t * emb, emb)] = (got[2 * t].astype(F32) + got[2 * t + 1].astype(F32)).astype(BF16)
    hidden += jnp.dot(pooled[...], w_first[pl.ds(0, table_width), :], preferred_element_type=F32)

    one = jnp.maximum(hidden, 0.0).astype(BF16)
    two = jnp.maximum(jnp.dot(one, w_second[...], preferred_element_type=F32), 0.0).astype(BF16)
    three = jnp.maximum(jnp.dot(two, w_third[...], preferred_element_type=F32), 0.0).astype(BF16)
    logit = jnp.sum(three.astype(F32) * w_out_ref[...].astype(F32), axis=1, keepdims=True)
    n_req, per_req = out_ref.shape
    row = lax.broadcasted_iota(jnp.int32, (n_rows, 128), 0) % per_req
    lane = lax.broadcasted_iota(jnp.int32, (n_rows, 128), 1)
    placed = jnp.where(row == lane, logit, 0.0).reshape(n_req, per_req, 128)
    out_ref[...] = jnp.sum(placed, axis=1)[:, :per_req]

    loop(1, n_cand, lambda step: send_back(step).wait_send())
    loop(1, at.chips, lambda step: send_sums(step).wait_send())


def on_device(
    n_grp, n_cand, history, lengths, target, bag_ids, leaf_ids, table_piece, leaf_table,
    w_query, w_key, w_pair, a_out, w_first, w_second, w_third, w_out,
):
    n_req, per_req, width = target.shape
    rows = n_req * per_req
    _, _, tables, bag = bag_ids.shape
    _, piece_rows, emb = table_piece.shape
    _, events, _ = history.shape
    trees, leaves, _ = leaf_table.shape
    att = w_pair.shape[1]
    chips = n_grp * n_cand // 2
    halves = chips // tables
    half_rows = 2 * piece_rows
    dma = pltpu.SemaphoreType.DMA
    hbm = pl.BlockSpec(memory_space=pl.ANY)
    vmem = pl.BlockSpec(memory_space=pltpu.VMEM)
    smem = pl.BlockSpec(memory_space=pltpu.SMEM)

    by_table = jnp.transpose(bag_ids.reshape(rows, tables, bag), (1, 0, 2)).reshape(tables, 1, rows * bag)
    half_of = jnp.arange(halves, dtype=jnp.int32).reshape(1, halves, 1)
    local = by_table - half_of * half_rows
    inside = (local >= 0) & (local < half_rows)
    ids = jnp.where(inside, local, half_rows).reshape(chips, 1, rows * bag)

    got_ids, cands, other_piece = pl.pallas_call(
        functools.partial(exchange_kernel, n_grp, n_cand),
        out_shape=(
            jax.ShapeDtypeStruct(ids.shape, jnp.int32),
            jax.ShapeDtypeStruct((n_cand, per_req, width), BF16),
            jax.ShapeDtypeStruct((piece_rows, emb), BF16),
        ),
        in_specs=[hbm] * 3,
        out_specs=(hbm,) * 3,
        scratch_shapes=[
            dma((chips,)), dma((chips,)), dma((n_cand,)), dma((n_cand,)), dma(()), dma(()), dma((2,)),
        ],
        compiler_params=pltpu.CompilerParams(collective_id=0, has_side_effects=True),
        name="exchange",
    )(ids, target, table_piece)

    sums = pl.pallas_call(
        functools.partial(pool_kernel, bag, rows),
        out_shape=jax.ShapeDtypeStruct((chips, rows, emb), BF16),
        in_specs=[smem, vmem, vmem],
        out_specs=vmem,
        scratch_shapes=[
            pltpu.VMEM((half_rows + 8, emb), F32),
            pltpu.VMEM((chips * rows, emb), F32),
        ],
        name="pool",
    )(got_ids.reshape(chips, rows * bag), table_piece, other_piece)

    return pl.pallas_call(
        functools.partial(score_kernel, n_grp, n_cand),
        out_shape=jax.ShapeDtypeStruct((n_req, per_req), F32),
        in_specs=[hbm, smem, vmem, vmem, vmem, hbm, hbm, vmem, vmem, vmem, vmem, hbm, hbm, hbm, vmem],
        out_specs=vmem,
        scratch_shapes=[
            pltpu.VMEM((chips, rows, emb), BF16),
            pltpu.VMEM((n_cand, per_req, width), F32),
            pltpu.VMEM((n_cand, per_req, width), F32),
            pltpu.VMEM((events, width), BF16),
            pltpu.VMEM((trees * leaves, width), BF16),
            pltpu.VMEM(w_first.shape, BF16),
            pltpu.VMEM(w_second.shape, BF16),
            pltpu.VMEM(w_third.shape, BF16),
            pltpu.VMEM((rows, events), F32),
            pltpu.VMEM((per_req * att, width), BF16),
            pltpu.VMEM((rows, tables * emb), BF16),
            dma((chips,)), dma((chips,)), dma((n_cand,)), dma((n_cand,)), dma((6,)),
        ],
        compiler_params=pltpu.CompilerParams(
            collective_id=1, has_side_effects=True, vmem_limit_bytes=56 * 1024 * 1024
        ),
        name="score",
    )(
        sums, lengths, cands, target.reshape(rows, width), leaf_ids.reshape(rows, trees), history,
        leaf_table.reshape(trees * leaves, width), w_query, w_key, w_pair, a_out.reshape(1, att),
        w_first, w_second, w_third, w_out.reshape(1, -1),
    )


def solution(mesh):
    n_grp, n_cand = mesh.shape["grp"], mesh.shape["cand"]
    both = ("grp", "cand")
    placed = (
        P(both, None, None), P(both), P("grp", "cand", None), P("grp", "cand", None, None),
        P("grp", "cand", None), P(both, None, None),
    ) + (P(),) * 9
    return jax.shard_map(
        functools.partial(on_device, n_grp, n_cand),
        mesh=mesh, in_specs=placed, out_specs=P("grp", "cand"), check_vma=False,
    )
```

time: 295 us -> 70.7 us (0.24)
  matrix products: 191 us -> 0 us
  Pallas kernels: 0 us -> 64.4 us
  blocking collectives: 25.6 us -> 0 us
  starting transfers between devices: 15.7 us -> 0 us
  local copies, waits for them, and re-layouts: 20.1 us -> 4.51 us
  between operations: 14.3 us -> 0.7 us
  waiting for transfers between devices: 9.95 us -> 0 us
  other arithmetic: 10.4 us -> 0.79 us
  loops' own time: 5.82 us -> 0 us
    dot_general x52 -> x0, matrix products: 191 us -> none  [the longest x8 132 us: add_block(): jnp.dot(counts, block_rows, preferred_element_type=jnp.float32)]
    pallas_call x0 -> x3, Pallas kernels: none -> 64.4 us  [the longest x1 26 us: on_device(): pl.pallas_call(functools.partial(score_kernel, n_grp, n_cand), out_shape=...]
    unnamed x1 -> x0, blocking collectives: 25.6 us -> none
    all_to_all x2 -> x0, starting transfers between devices: 15.7 us -> none  [the longest x1 11.5 us: on_device(): lax.all_to_all(outgoing, ('grp', 'cand'), split_axis=0, concat_axis=0, ti...]
    all_to_all x2 -> x0, waiting for transfers between devices: 9.24 us -> none  [the longest x1 9.24 us: on_device(): lax.all_to_all(outgoing, ('grp', 'cand'), split_axis=0, concat_axis=0, ti...]
    slice x9 -> x0, local copies, waits for them, and re-layouts: 8.4 us -> none  [the longest x1 7.66 us: on_device(): w_first[:table_width].reshape(tables, emb_width, -1)]
    another operation x2 -> x0, loops' own time: 5.82 us -> none  [the longest x1 5.76 us: on_device(): interest = lax.map(one_request, (target, history_all, lengths_all))]
    lt x8 -> x0, other arithmetic: 5.11 us -> none  [interest_of(): live_mask = jnp.arange(history_rows.shape[0], dtype=jnp.int32) < length]
  transfers between devices with their start and end apart: 3 -> 0, of which waited for: 1 -> 0; matrix products, arithmetic and copies ran while one was open for 52% -> 0% of each run, Pallas kernels for 0% -> 0%
where the time goes in v1:
time: 70.7 us; the launch traced here: 70.4 us
  Pallas kernels  64.4 us (91%)
  local copies, waits for them, and re-layouts  4.51 us (6%)
  other arithmetic  0.79 us (1%)
    pallas_call x1, Pallas kernels, on_device(): pl.pallas_call(functools.partial(score_kernel, n_grp, n_cand), out_shape=...  26 us
    pallas_call x1, Pallas kernels, on_device(): pl.pallas_call(functools.partial(pool_kernel, bag, rows), out_shape=jax.S...  21.7 us
    pallas_call x1, Pallas kernels, on_device(): pl.pallas_call(functools.partial(exchange_kernel, n_grp, n_cand), out_sha...  16.7 us
    unnamed x4, local copies, waits for them, and re-layouts  2.74 us

profile of v1, /device:TPU:1, one launch (start us, length us, event | category | flops | bytes accessed | tf_op | source)
XLA Modules:
  0.0 70.4 jit_solution(4505222241364494436)
XLA Ops:
  0.0 1.0 %copy.17 = s32[32,256]{1,0:T(8,128)S(1)} copy(s32[32,256]{0,1:T(8,128)} %bitcast.15) | data formatting | bytes 65536 | tf_op jit(solution)/shard_map/sub | solution.py:327
  1.0 0.1 sub.30
  1.1 0.1 sub.32
  1.2 0.8 %and_select_fusion.ids_ref = s32[64,1,256]{2,1,0:T(1,128)} fusion(s32[64,1,256]{2,1,0:T(1,128)S(1)} %sub.30, s32[64]{0:T(128)S(1)} %sub.32), kind=kLoop, calls=%fused_computation | loop fusion | flops 81920 | bytes 131328 | tf_op jit(solution)/shard_map/jit(_where)/select_n | solution.py:329
  2.0 16.7 %exchange.1 = (s32[64,1,256]{2,1,0:T(1,128)}, bf16[8,8,256]{2,1,0:T(8,128)(2,1)}, bf16[8192,128]{1,0:T(8,128)(2,1)}) custom-call(s32[64,1,256]{2,1,0:T(1,128)} %and_select_fusion.ids_ref, bf16[8,8,256]{2,1,0:T(8,128)(2,1)} %target_ref.1, bf16[1,8192,128]{2,1,0:T(8,128)(2,1)} %own_ref.1), custom_call_target="tpu_custom_call" | custom-call | tf_op jit(solution)/shard_map/exchange/pallas_call | solution.py:331
  18.7 1.5 %copy.20 = s32[64,1,256]{2,0,1:T(8,128)} copy(s32[64,1,256]{2,1,0:T(1,128)} %get-tuple-element.8) | data formatting | bytes 131072
  20.1 0.0 copy-start
  20.1 21.7 %pool.1.sums_ref = bf16[64,64,128]{2,1,0:T(8,128)(2,1)} custom-call(s32[64,256]{1,0:T(8,128)} %bitcast.13, bf16[1,8192,128]{2,1,0:T(8,128)(2,1)} %own_ref.1, bf16[8192,128]{1,0:T(8,128)(2,1)} %get-tuple-element.9.other_ref), custom_call_target="tpu_custom_call" | custom-call | tf_op jit(solution)/shard_map/pool/pallas_call | solution.py:347
  41.9 0.0 copy-done
  41.9 0.6 reshape.82.w_out_ref
  43.1 26.0 %score.1 = f32[8,8]{1,0:T(8,128)} custom-call(bf16[64,64,128]{2,1,0:T(8,128)(2,1)} %pool.1.sums_ref, s32[1]{0:T(128)S(6)} %copy.22.length_ref, bf16[8,8,256]{2,1,0:T(8,128)(2,1)} %get-tuple-element.10.cands_ref, bf16[64,256]{1,0:T(8,128)(2,1)} %bitcast.14, s32[64,64]{1,0:T(8,128)} %bitcast.16, bf16[1,1024,256]{2,1,0:T(8,128)(2,1)} %history_hbm.1, ...), custom_call_target="tpu_custom_call" | custom-call | tf_op jit(solution)/shard_map/score/pallas_call | solution.py:359
  69.1 1.3 %copy.23 = f32[8,8]{1,0:T(8,128)} copy(f32[8,8]{1,0:T(8,128)} %score.1) | data formatting | bytes 512
  (3 shorter events, 0.0 us)
Async XLA Ops:
  20.1 21.7 %copy-start = (bf16[256]{0:T(256)(128)(2,1)S(1)}, bf16[256]{0:T(256)(128)(2,1)}, u32[]{:S(2)}) copy-start(bf16[256]{0:T(256)(128)(2,1)} %param.29) | copy-start | bytes 1540

commit v2 on v1

v2 whole, which is shorter than its diff:
```python
import functools

import jax
import jax.numpy as jnp
from jax import lax
from jax.experimental import pallas as pl
from jax.experimental.pallas import tpu as pltpu
from jax.sharding import PartitionSpec as P

MESH = pl.DeviceIdType.MESH
PARTS = 4
STRIDE = 27
F32 = jnp.float32
BF16 = jnp.bfloat16


class Place:
    def __init__(self, n_grp, n_cand):
        self.n_cand = n_cand
        self.chips_x = n_cand // 2
        self.chips = n_grp * self.chips_x
        self.grp = lax.axis_index("grp")
        self.cand = lax.axis_index("cand")
        self.core = lax.rem(self.cand, 2)
        self.x = lax.div(self.cand, 2)
        self.chip = self.grp * self.chips_x + self.x

    def same_core(self, chip):
        return (lax.div(chip, self.chips_x), 2 * lax.rem(chip, self.chips_x) + self.core)

    def other_core(self, step):
        return (self.grp, 2 * lax.rem(self.x + step, self.chips_x) + 1 - self.core)

    def chip_after(self, step):
        return lax.rem(self.chip + step, self.chips)

    def enter(self):
        barrier = pltpu.get_barrier_semaphore()

        def greet_same(step, carry):
            pl.semaphore_signal(
                barrier, inc=1, device_id=self.same_core(self.chip_after(step)), device_id_type=MESH
            )
            return carry

        lax.fori_loop(1, self.chips, greet_same, 0)
        for step in range(self.chips_x):
            pl.semaphore_signal(barrier, inc=1, device_id=self.other_core(step), device_id_type=MESH)
        return barrier, self.chips - 1 + self.chips_x


def repeat(first, last, act):
    def body(step, carry):
        act(step)
        return carry

    lax.fori_loop(first, last, body, 0)


def kernel(
    n_grp, n_cand, bag_hbm, length_hbm, target_hbm, rows_hbm, leaf_ids_hbm, history_hbm, leaf_hbm, piece_hbm,
    w_query_hbm, w_key_hbm, w_pair_hbm, a_out_hbm, w_first_hbm, w_second_hbm, w_third_hbm, w_out_hbm,
    out_ref,
    bags, length_s, target, target_rows, leaf_ids, history, leaf_table, own, w_query, w_key, w_pair, a_out,
    w_first, w_second, w_third, w_out,
    ids_stage, ids_got, ids_s, other, table, total, sums, got, cands, back, interest, scores, comb, pooled, hidden_ref,
    load_sem, ids_send, ids_recv, ids_sem, swap_send, swap_recv, t_send, t_recv,
    sum_send, sum_recv, back_send, back_recv,
):
    at = Place(n_grp, n_cand)
    barrier, count = at.enter()
    pairs = dict(
        bags=(bag_hbm, bags), own=(piece_hbm.at[0], own), target=(target_hbm, target),
        w_pair=(w_pair_hbm, w_pair), w_key=(w_key_hbm, w_key), w_query=(w_query_hbm, w_query),
        a_out=(a_out_hbm, a_out), history=(history_hbm.at[0], history), leaf_ids=(leaf_ids_hbm, leaf_ids),
        leaf=(leaf_hbm, leaf_table), rows=(rows_hbm, target_rows), length=(length_hbm, length_s),
        w_first=(w_first_hbm, w_first), w_second=(w_second_hbm, w_second), w_third=(w_third_hbm, w_third),
        w_out=(w_out_hbm, w_out),
    )
    loads = {
        name: pltpu.make_async_copy(src, dst, load_sem.at[i])
        for i, (name, (src, dst)) in enumerate(pairs.items())
    }
    for load in loads.values():
        load.start()

    n_rows, bag, tables = bags.shape
    piece_rows, emb = other.shape
    half_rows = 2 * piece_rows
    halves = at.chips // tables
    parts = PARTS
    part = piece_rows // parts

    loads["bags"].wait()
    turned = [bags[:, slot, :].T for slot in range(bag)]
    for half in range(halves):
        for slot in range(0, bag, 2):
            both = jnp.concatenate(turned[slot : slot + 2], axis=1) - half * half_rows
            both = jnp.where((both >= 0) & (both < half_rows), both, half_rows)
            ids_stage[half, :, 0, pl.ds(slot * n_rows, 2 * n_rows)] = both

    def send_ids(step):
        to = at.chip_after(step)
        return pltpu.make_async_remote_copy(
            src_ref=ids_stage.at[lax.rem(to, halves), lax.div(to, halves)], dst_ref=ids_got.at[at.chip],
            send_sem=ids_send.at[step], recv_sem=ids_recv.at[at.chip],
            device_id=at.same_core(to), device_id_type=MESH,
        )

    def ids_from(step):
        chip = at.chip_after(step)
        return pltpu.make_async_remote_copy(
            src_ref=ids_stage.at[0, 0], dst_ref=ids_got.at[chip],
            send_sem=ids_send.at[step], recv_sem=ids_recv.at[chip],
            device_id=at.same_core(chip), device_id_type=MESH,
        )

    def send_target(step):
        to = lax.rem(at.cand + step, n_cand)
        return pltpu.make_async_remote_copy(
            src_ref=target.at[to], dst_ref=cands.at[at.cand],
            send_sem=t_send.at[step], recv_sem=t_recv.at[at.cand],
            device_id=(at.grp, to), device_id_type=MESH,
        )

    def target_from(step):
        cand = lax.rem(at.cand + step, n_cand)
        return pltpu.make_async_remote_copy(
            src_ref=target.at[cand], dst_ref=cands.at[cand],
            send_sem=t_send.at[step], recv_sem=t_recv.at[cand],
            device_id=(at.grp, cand), device_id_type=MESH,
        )

    def swap(i):
        rows = pl.ds(i * part, part)
        return pltpu.make_async_remote_copy(
            src_ref=own.at[rows], dst_ref=other.at[rows],
            send_sem=swap_send.at[i], recv_sem=swap_recv.at[i],
            device_id=at.other_core(0), device_id_type=MESH,
        )

    def source(step):
        return at.chip_after(lax.rem(step * STRIDE, at.chips))

    def send_sums(step):
        to = source(step)
        return pltpu.make_async_remote_copy(
            src_ref=sums.at[to], dst_ref=got.at[at.chip],
            send_sem=sum_send.at[step], recv_sem=sum_recv.at[at.chip],
            device_id=at.same_core(to), device_id_type=MESH,
        )

    def sums_from(step):
        chip = at.chip_after(step)
        return pltpu.make_async_remote_copy(
            src_ref=sums.at[chip], dst_ref=got.at[chip],
            send_sem=sum_send.at[step], recv_sem=sum_recv.at[chip],
            device_id=at.same_core(chip), device_id_type=MESH,
        )

    def send_back(step):
        to = lax.rem(at.cand + step, n_cand)
        return pltpu.make_async_remote_copy(
            src_ref=interest.at[to], dst_ref=back.at[at.cand],
            send_sem=back_send.at[step], recv_sem=back_recv.at[at.cand],
            device_id=(at.grp, to), device_id_type=MESH,
        )

    def back_from(step):
        cand = lax.rem(at.cand + step, n_cand)
        return pltpu.make_async_remote_copy(
            src_ref=interest.at[cand], dst_ref=back.at[cand],
            send_sem=back_send.at[step], recv_sem=back_recv.at[cand],
            device_id=(at.grp, cand), device_id_type=MESH,
        )

    chunk = 512

    def widen(piece, core, first, rows):
        def step(i):
            here = pl.multiple_of(first + i * chunk, chunk)
            there = pl.multiple_of(core * piece_rows + first + i * chunk, chunk)
            table[pl.ds(there, chunk), :] = piece[pl.ds(here, chunk), :].astype(F32)

        repeat(0, rows // chunk, step)

    loads["own"].wait()
    widen(own, at.core, 0, piece_rows)
    table[pl.ds(half_rows, 8), :] = jnp.zeros((8, emb), F32)
    total[...] = jnp.zeros_like(total)
    loads["target"].wait()
    cands[at.cand] = target[at.cand]
    ids_got[at.chip] = ids_stage[lax.rem(at.chip, halves), lax.div(at.chip, halves)]
    for name in ("w_pair", "w_key", "w_query", "a_out", "history"):
        loads[name].wait()
    events, width = history.shape
    att = w_pair.shape[1]
    per_src = cands.shape[1]
    pair_t = w_pair[...].astype(F32).T
    key_t = w_key[...].astype(F32).T
    query_t = w_query[...].astype(F32).T.astype(BF16)
    a_col = a_out[...].astype(F32).T
    a_wide = jnp.broadcast_to(a_col, (att, 256))
    history_t = history[...].astype(F32).T.astype(BF16)

    pl.semaphore_wait(barrier, count)
    repeat(1, at.chips, lambda step: send_ids(step).start())
    repeat(1, n_cand, lambda step: send_target(step).start())
    for i in range(parts):
        swap(i).start()

    for name in ("leaf_ids", "leaf", "rows", "length", "w_first"):
        loads[name].wait()
    trees = leaf_ids.shape[1]
    leaves = leaf_table.shape[0] // trees
    spread_row = lax.broadcasted_iota(jnp.int32, (trees, trees * leaves), 0)
    spread_col = lax.broadcasted_iota(jnp.int32, (trees, trees * leaves), 1)
    spread = (spread_row == spread_col // leaves).astype(F32).astype(BF16)
    wide = jnp.dot(leaf_ids[...].astype(F32).astype(BF16), spread, preferred_element_type=F32)
    leaf_of = lax.broadcasted_iota(jnp.int32, wide.shape, 1) % leaves
    hot = (wide == leaf_of.astype(F32)).astype(F32).astype(BF16)
    leaf_vec = jnp.dot(hot, leaf_table[...], preferred_element_type=F32).astype(BF16)
    table_width = w_first.shape[0] - 3 * width
    hidden_ref[...] = jnp.dot(
        target_rows[...], w_first[pl.ds(table_width + width, width), :], preferred_element_type=F32
    ) + jnp.dot(leaf_vec, w_first[pl.ds(table_width + 2 * width, width), :], preferred_element_type=F32)

    repeat(1, n_cand, lambda step: target_from(step).wait_recv())
    length = length_s[0]

    def one_group(g):
        rows_f = cands[g].astype(F32)
        q_part = lax.dot_general(query_t, cands[g], (((1,), (1,)), ((), ())), preferred_element_type=F32)
        base = jnp.sum(q_part * a_col, axis=0, keepdims=True)
        for c in range(per_src):
            comb[pl.ds(c * att, att), :] = (rows_f[c : c + 1, :] * pair_t + key_t).astype(BF16)
        for block in range(events // 256):
            cols = pl.ds(block * 256, 256)
            raw = jnp.dot(comb[...], history_t[:, block * 256 : block * 256 + 256], preferred_element_type=F32)
            for c in range(per_src):
                unit = jnp.maximum(raw[c * att : (c + 1) * att, :], -q_part[:, c : c + 1]) * a_wide
                line = jnp.sum(unit, axis=0, keepdims=True) + base[:, c : c + 1]
                scores[pl.ds(g * per_src + c, 1), cols] = line

    repeat(0, n_cand, one_group)
    live = lax.broadcasted_iota(jnp.int32, scores.shape, 1) < length
    weights = jnp.where(live, scores[...], 0.0).astype(BF16)
    weighted = jnp.dot(weights, history[...], preferred_element_type=F32)
    root = jnp.sqrt(jnp.full((1, 1), length, jnp.int32).astype(F32))
    weighted = weighted * (1.0 / root)
    interest[...] = weighted.reshape(interest.shape)

    repeat(1, at.chips, lambda step: ids_from(step).wait_recv())
    to_scalar = pltpu.make_async_copy(ids_got, ids_s, ids_sem)
    to_scalar.start()
    for i in range(parts):
        swap(i).wait_recv()
        widen(other, 1 - at.core, i * part, part)
    back[at.cand] = interest[at.cand]
    repeat(1, n_cand, lambda step: send_back(step).start())
    to_scalar.wait()

    def one_source(step):
        src = source(step)

        @pl.when(step >= 3)
        def _():
            send_sums(step - 2).start()

        sums[source(step + at.chips - 1)] = total[...].astype(BF16)
        for row in range(n_rows):
            row_sum = None
            for slot in range(bag):
                line = table[pl.ds(ids_s[src, 0, slot * n_rows + row], 1), :]
                row_sum = line if row_sum is None else row_sum + line
            total[pl.ds(row, 1), :] = row_sum

    repeat(0, at.chips, one_source)
    sums[source(at.chips - 1)] = total[...].astype(BF16)
    send_sums(at.chips - 2).start()
    got[at.chip] = sums[at.chip]
    repeat(1, n_cand, lambda step: back_from(step).wait_recv())
    seen = back[...].reshape(n_rows, width).astype(BF16)
    hidden = hidden_ref[...] + jnp.dot(seen, w_first[pl.ds(table_width, width), :], preferred_element_type=F32)
    send_sums(at.chips - 1).start()
    for name in ("w_second", "w_third", "w_out"):
        loads[name].wait()
    repeat(1, at.chips, lambda step: sums_from(step).wait_recv())
    for t in range(tables):
        pooled[:, pl.ds(t * emb, emb)] = (got[2 * t].astype(F32) + got[2 * t + 1].astype(F32)).astype(BF16)
    hidden += jnp.dot(pooled[...], w_first[pl.ds(0, table_width), :], preferred_element_type=F32)
    one = jnp.maximum(hidden, 0.0).astype(BF16)
    two = jnp.maximum(jnp.dot(one, w_second[...], preferred_element_type=F32), 0.0).astype(BF16)
    three = jnp.maximum(jnp.dot(two, w_third[...], preferred_element_type=F32), 0.0).astype(BF16)
    logit = jnp.sum(three.astype(F32) * w_out[...].astype(F32), axis=1, keepdims=True)
    n_req, per_req = out_ref.shape
    row = lax.broadcasted_iota(jnp.int32, (n_rows, 128), 0) % per_req
    lane = lax.broadcasted_iota(jnp.int32, (n_rows, 128), 1)
    placed = jnp.where(row == lane, logit, 0.0).reshape(n_req, per_req, 128)
    out_ref[...] = jnp.sum(placed, axis=1)[:, :per_req]

    repeat(1, at.chips, lambda step: send_ids(step).wait_send())
    repeat(1, n_cand, lambda step: send_target(step).wait_send())
    for i in range(parts):
        swap(i).wait_send()
    repeat(1, n_cand, lambda step: send_back(step).wait_send())
    repeat(1, at.chips, lambda step: send_sums(step).wait_send())


def on_device(
    n_grp, n_cand, history, lengths, target, bag_ids, leaf_ids, table_piece, leaf_table,
    w_query, w_key, w_pair, a_out, w_first, w_second, w_third, w_out,
):
    n_req, per_req, width = target.shape
    rows = n_req * per_req
    _, _, tables, bag = bag_ids.shape
    _, piece_rows, emb = table_piece.shape
    _, events, _ = history.shape
    trees, leaves, _ = leaf_table.shape
    att = w_pair.shape[1]
    chips = n_grp * n_cand // 2
    halves = chips // tables
    dma = pltpu.SemaphoreType.DMA
    hbm = pl.BlockSpec(memory_space=pl.ANY)

    args = (
        jnp.transpose(bag_ids, (0, 1, 3, 2)).reshape(rows, bag, tables), lengths, target,
        target.reshape(rows, width), leaf_ids.reshape(rows, trees), history,
        leaf_table.reshape(trees * leaves, width), table_piece, w_query, w_key, w_pair, a_out.reshape(1, att),
        w_first, w_second, w_third, w_out.reshape(1, -1),
    )

    def held(i):
        return pltpu.VMEM(args[i].shape, args[i].dtype)

    return pl.pallas_call(
        functools.partial(kernel, n_grp, n_cand),
        out_shape=jax.ShapeDtypeStruct((n_req, per_req), F32),
        in_specs=[hbm] * len(args),
        out_specs=pl.BlockSpec(memory_space=pltpu.VMEM),
        scratch_shapes=[
            held(0), pltpu.SMEM((1,), jnp.int32), held(2), held(3), held(4), pltpu.VMEM((events, width), BF16),
            held(6), pltpu.VMEM((piece_rows, emb), BF16), held(8), held(9), held(10), held(11),
            held(12), held(13), held(14), held(15),
            pltpu.VMEM((halves, tables, 1, rows * bag), jnp.int32),
            pltpu.VMEM((chips, 1, rows * bag), jnp.int32),
            pltpu.SMEM((chips, 1, rows * bag), jnp.int32),
            pltpu.VMEM((piece_rows, emb), BF16),
            pltpu.VMEM((2 * piece_rows + 8, emb), F32),
            pltpu.VMEM((rows, emb), F32),
            pltpu.VMEM((chips, rows, emb), BF16),
            pltpu.VMEM((chips, rows, emb), BF16),
            pltpu.VMEM((n_cand, per_req, width), BF16),
            pltpu.VMEM((n_cand, per_req, width), F32),
            pltpu.VMEM((n_cand, per_req, width), F32),
            pltpu.VMEM((rows, events), F32),
            pltpu.VMEM((per_req * att, width), BF16),
            pltpu.VMEM((rows, tables * emb), BF16),
            pltpu.VMEM((rows, w_first.shape[1]), F32),
            dma((len(args),)), dma((chips,)), dma((chips,)), dma(()), dma((PARTS,)), dma((PARTS,)),
            dma((n_cand,)), dma((n_cand,)), dma((chips,)), dma((chips,)), dma((n_cand,)), dma((n_cand,)),
        ],
        compiler_params=pltpu.CompilerParams(
            collective_id=0, has_side_effects=True, vmem_limit_bytes=56 * 1024 * 1024
        ),
        name="rank",
    )(*args)


def solution(mesh):
    n_grp, n_cand = mesh.shape["grp"], mesh.shape["cand"]
    both = ("grp", "cand")
    placed = (
        P(both, None, None), P(both), P("grp", "cand", None), P("grp", "cand", None, None),
        P("grp", "cand", None), P(both, None, None),
    ) + (P(),) * 9
    return jax.shard_map(
        functools.partial(on_device, n_grp, n_cand),
        mesh=mesh, in_specs=placed, out_specs=P("grp", "cand"), check_vma=False,
    )
```

time: 70.7 us -> 52.8 us (0.75)
  Pallas kernels: 64.4 us -> 49.5 us
  local copies, waits for them, and re-layouts: 4.51 us -> 2.5 us
  other arithmetic: 0.79 us -> 0 us
    pallas_call x3 -> x1, Pallas kernels: 64.4 us -> 49.5 us  [on_device(): pl.pallas_call(functools.partial(kernel, n_grp, n_cand), out_shape=jax.Sh...]
    unnamed x4 -> x1, local copies, waits for them, and re-layouts: 2.74 us -> 1.28 us
    sub x5 -> x0, local copies, waits for them, and re-layouts: 1.2 us -> none  [on_device(): local = by_table - half_of * half_rows]
    select_n x1 -> x0, other arithmetic: 0.78 us -> none  [on_device(): ids = jnp.where(inside, local, half_rows).reshape(chips, 1, rows * bag)]
where the time goes in v2:
time: 52.8 us; the launch traced here: 52.7 us
  Pallas kernels  49.5 us (94%)
  local copies, waits for them, and re-layouts  2.5 us (5%)
  between operations  0.66 us (1%)
    pallas_call x1, Pallas kernels, on_device(): pl.pallas_call(functools.partial(kernel, n_grp, n_cand), out_shape=jax.Sh...  49.5 us
    unnamed x1, local copies, waits for them, and re-layouts  1.28 us
    reshape x1, local copies, waits for them, and re-layouts, on_device(): w_out.reshape(1, -1)  1.22 us

profile of v2, /device:TPU:1, one launch (start us, length us, event | category | flops | bytes accessed | tf_op | source)
XLA Modules:
  0.0 52.7 jit_solution(2197376515381722029)
XLA Ops:
  0.7 1.2 %reshape.23.w_out_hbm = bf16[1,256]{1,0:T(2,128)(2,1)} reshape(bf16[256]{0:T(256)(128)(2,1)} %param.29) | data formatting | bytes 1024 | tf_op jit(solution)/shard_map/reshape | solution.py:330
  1.9 49.5 %rank.1 = f32[8,8]{1,0:T(8,128)} custom-call(s32[64,4,32]{2,1,0:T(4,128)} %bitcast.8, s32[1]{0:T(128)S(6)} %copy.17.length_hbm, bf16[8,8,256]{2,1,0:T(8,128)(2,1)} %target_hbm.1, bf16[64,256]{1,0:T(8,128)(2,1)} %bitcast.9, s32[64,64]{1,0:T(8,128)} %bitcast.10, bf16[1,1024,256]{2,1,0:T(8,128)(2,1)} %history_hbm.1, bf16[2048,256]{1,0:T(8,128)(2,1)} %bitcast.7, ...), custom_call_target="tpu_custom_call" | custom-call | tf_op jit(solution)/shard_map/rank/pallas_call | solution.py:336
  51.4 1.3 %copy.18 = f32[8,8]{1,0:T(8,128)} copy(f32[8,8]{1,0:T(8,128)} %rank.1) | data formatting | bytes 512

commit v3 on v2

--- a/solution.py
+++ b/solution.py
@@ -1,4 +1,5 @@
 import functools
+import math
 
 import jax
 import jax.numpy as jnp
@@ -9,41 +10,70 @@
 
 MESH = pl.DeviceIdType.MESH
 PARTS = 4
-STRIDE = 27
+EARLY = 3
 F32 = jnp.float32
 BF16 = jnp.bfloat16
 
 
 class Place:
     def __init__(self, n_grp, n_cand):
-        self.n_cand = n_cand
+        self.side = math.isqrt(n_grp)
         self.chips_x = n_cand // 2
         self.chips = n_grp * self.chips_x
         self.grp = lax.axis_index("grp")
         self.cand = lax.axis_index("cand")
         self.core = lax.rem(self.cand, 2)
         self.x = lax.div(self.cand, 2)
+        self.z = lax.div(self.grp, self.side)
         self.chip = self.grp * self.chips_x + self.x
-
-    def same_core(self, chip):
-        return (lax.div(chip, self.chips_x), 2 * lax.rem(chip, self.chips_x) + self.core)
+        y = lax.rem(self.grp, self.side)
+        self.ys = [lax.rem(y + dy, self.side) for dy in range(self.side)]
+        self.xs = [lax.rem(self.x + dx, self.chips_x) for dx in range(self.chips_x)]
+        far_y = sorted(range(self.side), key=lambda d: -min(d, self.side - d))
+        far_x = sorted(range(self.chips_x), key=lambda d: -min(d, self.chips_x - d))
+        self.steps = [(dy, dx) for dy in far_y for dx in far_x]
+
+    def plane(self, j):
+        dz = 2 - j + 3 * (j // 2) - 2 * (j // 3) if isinstance(j, int) else (
+            2 - j + 3 * lax.div(j, 2) - 2 * lax.div(j, 3)
+        )
+        return lax.rem(self.z + dz, self.side) * self.side
+
+    def plane_from(self, j):
+        dz = 2 + j - 3 * lax.div(j, 2) + 2 * lax.div(j, 3)
+        return lax.rem(self.z + dz, self.side) * self.side
+
+    def chip_in(self, plane, i):
+        dy, dx = self.steps[i]
+        return (plane + self.ys[dy]) * self.chips_x + self.xs[dx]
+
+    def same_core(self, plane, i):
+        dy, dx = self.steps[i]
+        return (plane + self.ys[dy], 2 * self.xs[dx] + self.core)
 
     def other_core(self, step):
-        return (self.grp, 2 * lax.rem(self.x + step, self.chips_x) + 1 - self.core)
+        return (self.grp, 2 * self.xs[step] + 1 - self.core)
 
     def chip_after(self, step):
         return lax.rem(self.chip + step, self.chips)
 
+    def each_other_chip(self, act):
+        def far(j):
+            plane = self.plane(j)
+            for i in range(len(self.steps)):
+                act(plane, i)
+
+        repeat(0, self.side - 1, far)
+        for i in range(len(self.steps) - 1):
+            act(self.grp - self.ys[0], i)
+
     def enter(self):
         barrier = pltpu.get_barrier_semaphore()
-
-        def greet_same(step, carry):
-            pl.semaphore_signal(
-                barrier, inc=1, device_id=self.same_core(self.chip_after(step)), device_id_type=MESH
+        self.each_other_chip(
+            lambda plane, i: pl.semaphore_signal(
+                barrier, inc=1, device_id=self.same_core(plane, i), device_id_type=MESH
             )
-            return carry
-
-        lax.fori_loop(1, self.chips, greet_same, 0)
+        )
         for step in range(self.chips_x):
             pl.semaphore_signal(barrier, inc=1, device_id=self.other_core(step), device_id_type=MESH)
         return barrier, self.chips - 1 + self.chips_x
@@ -97,23 +127,27 @@
         for slot in range(0, bag, 2):
             both = jnp.concatenate(turned[slot : slot + 2], axis=1) - half * half_rows
             both = jnp.where((both >= 0) & (both < half_rows), both, half_rows)
-            ids_stage[half, :, 0, pl.ds(slot * n_rows, 2 * n_rows)] = both
-
-    def send_ids(step):
-        to = at.chip_after(step)
-        return pltpu.make_async_remote_copy(
-            src_ref=ids_stage.at[lax.rem(to, halves), lax.div(to, halves)], dst_ref=ids_got.at[at.chip],
-            send_sem=ids_send.at[step], recv_sem=ids_recv.at[at.chip],
-            device_id=at.same_core(to), device_id_type=MESH,
-        )
-
-    def ids_from(step):
-        chip = at.chip_after(step)
+            ids_stage[:, half, 0, pl.ds(slot * n_rows, 2 * n_rows)] = both
+
+    def staged(chip):
+        return ids_stage.at[lax.div(chip, halves), lax.rem(chip, halves)]
+
+    def send_ids(plane, i):
+        to = at.chip_in(plane, i)
+        return pltpu.make_async_remote_copy(
+            src_ref=staged(to), dst_ref=ids_got.at[at.chip],
+            send_sem=ids_send.at[to], recv_sem=ids_recv.at[at.chip],
+            device_id=at.same_core(plane, i), device_id_type=MESH,
+        )
+
+    def ids_of(chip):
         return pltpu.make_async_remote_copy(
             src_ref=ids_stage.at[0, 0], dst_ref=ids_got.at[chip],
-            send_sem=ids_send.at[step], recv_sem=ids_recv.at[chip],
-            device_id=at.same_core(chip), device_id_type=MESH,
-        )
+            send_sem=ids_send.at[chip], recv_sem=ids_recv.at[chip],
+            device_id=at.other_core(0), device_id_type=MESH,
+        )
+
+    own_ids = pltpu.make_async_copy(staged(at.chip), ids_got.at[at.chip], ids_recv.at[at.chip])
 
     def send_target(step):
         to = lax.rem(at.cand + step, n_cand)
@@ -139,23 +173,19 @@
             device_id=at.other_core(0), device_id_type=MESH,
         )
 
-    def source(step):
-        return at.chip_after(lax.rem(step * STRIDE, at.chips))
-
-    def send_sums(step):
-        to = source(step)
+    def send_sums(plane, i):
+        to = at.chip_in(plane, i)
         return pltpu.make_async_remote_copy(
             src_ref=sums.at[to], dst_ref=got.at[at.chip],
-            send_sem=sum_send.at[step], recv_sem=sum_recv.at[at.chip],
-            device_id=at.same_core(to), device_id_type=MESH,
-        )
-
-    def sums_from(step):
-        chip = at.chip_after(step)
+            send_sem=sum_send.at[to], recv_sem=sum_recv.at[at.chip],
+            device_id=at.same_core(plane, i), device_id_type=MESH,
+        )
+
+    def sums_of(chip):
         return pltpu.make_async_remote_copy(
             src_ref=sums.at[chip], dst_ref=got.at[chip],
-            send_sem=sum_send.at[step], recv_sem=sum_recv.at[chip],
-            device_id=at.same_core(chip), device_id_type=MESH,
+            send_sem=sum_send.at[chip], recv_sem=sum_recv.at[chip],
+            device_id=at.other_core(0), device_id_type=MESH,
         )
 
     def send_back(step):
@@ -187,10 +217,8 @@
     loads["own"].wait()
     widen(own, at.core, 0, piece_rows)
     table[pl.ds(half_rows, 8), :] = jnp.zeros((8, emb), F32)
-    total[...] = jnp.zeros_like(total)
     loads["target"].wait()
     cands[at.cand] = target[at.cand]
-    ids_got[at.chip] = ids_stage[lax.rem(at.chip, halves), lax.div(at.chip, halves)]
     for name in ("w_pair", "w_key", "w_query", "a_out", "history"):
         loads[name].wait()
     events, width = history.shape
@@ -203,32 +231,8 @@
     a_wide = jnp.broadcast_to(a_col, (att, 256))
     history_t = history[...].astype(F32).T.astype(BF16)
 
-    pl.semaphore_wait(barrier, count)
-    repeat(1, at.chips, lambda step: send_ids(step).start())
-    repeat(1, n_cand, lambda step: send_target(step).start())
-    for i in range(parts):
-        swap(i).start()
-
-    for name in ("leaf_ids", "leaf", "rows", "length", "w_first"):
-        loads[name].wait()
-    trees = leaf_ids.shape[1]
-    leaves = leaf_table.shape[0] // trees
-    spread_row = lax.broadcasted_iota(jnp.int32, (trees, trees * leaves), 0)
-    spread_col = lax.broadcasted_iota(jnp.int32, (trees, trees * leaves), 1)
-    spread = (spread_row == spread_col // leaves).astype(F32).astype(BF16)
-    wide = jnp.dot(leaf_ids[...].astype(F32).astype(BF16), spread, preferred_element_type=F32)
-    leaf_of = lax.broadcasted_iota(jnp.int32, wide.shape, 1) % leaves
-    hot = (wide == leaf_of.astype(F32)).astype(F32).astype(BF16)
-    leaf_vec = jnp.dot(hot, leaf_table[...], preferred_element_type=F32).astype(BF16)
-    table_width = w_first.shape[0] - 3 * width
-    hidden_ref[...] = jnp.dot(
-        target_rows[...], w_first[pl.ds(table_width + width, width), :], preferred_element_type=F32
-    ) + jnp.dot(leaf_vec, w_first[pl.ds(table_width + 2 * width, width), :], preferred_element_type=F32)
-
-    repeat(1, n_cand, lambda step: target_from(step).wait_recv())
-    length = length_s[0]
-
-    def one_group(g):
+    def one_group(step):
+        g = lax.rem(at.cand + step, n_cand)
         rows_f = cands[g].astype(F32)
         q_part = lax.dot_general(query_t, cands[g], (((1,), (1,)), ((), ())), preferred_element_type=F32)
         base = jnp.sum(q_part * a_col, axis=0, keepdims=True)
@@ -242,7 +246,76 @@
                 line = jnp.sum(unit, axis=0, keepdims=True) + base[:, c : c + 1]
                 scores[pl.ds(g * per_src + c, 1), cols] = line
 
-    repeat(0, n_cand, one_group)
+    def arrived_group(step):
+        target_from(step).wait_recv()
+        one_group(step)
+
+    one_group(0)
+
+    pl.semaphore_wait(barrier, count)
+    repeat(1, n_cand, lambda step: send_target(step).start())
+    at.each_other_chip(lambda plane, i: send_ids(plane, i).start())
+    own_ids.start()
+    for i in range(parts):
+        swap(i).start()
+
+    for name in ("leaf_ids", "leaf"):
+        loads[name].wait()
+    trees = leaf_ids.shape[1]
+    leaves = leaf_table.shape[0] // trees
+    spread_row = lax.broadcasted_iota(jnp.int32, (trees, trees * leaves), 0)
+    spread_col = lax.broadcasted_iota(jnp.int32, (trees, trees * leaves), 1)
+    spread = (spread_row == spread_col // leaves).astype(F32).astype(BF16)
+    wide = jnp.dot(leaf_ids[...].astype(F32).astype(BF16), spread, preferred_element_type=F32)
+    leaf_of = lax.broadcasted_iota(jnp.int32, wide.shape, 1) % leaves
+    hot = (wide == leaf_of.astype(F32)).astype(F32).astype(BF16)
+    leaf_vec = jnp.dot(hot, leaf_table[...], preferred_element_type=F32).astype(BF16)
+    repeat(1, EARLY, arrived_group)
+
+    def to_scalar(chip, i):
+        return pltpu.make_async_copy(ids_got.at[chip], ids_s.at[i], ids_sem.at[i])
+
+    def fetch(plane, first, last):
+        for i in range(first, last):
+            chip = at.chip_in(plane, i)
+            ids_of(chip).wait_recv()
+            to_scalar(chip, i).start()
+
+    in_plane = len(at.steps)
+    batch = 4
+    fetch(at.plane(0), 0, in_plane)
+    for i in range(parts):
+        swap(i).wait_recv()
+        widen(other, 1 - at.core, i * part, part)
+
+    def one_plane(j):
+        plane = at.plane(j)
+        for i in range(in_plane):
+            chip = at.chip_in(plane, i)
+            to_scalar(chip, i).wait()
+            for row in range(n_rows):
+                row_sum = None
+                for slot in range(bag):
+                    line = table[pl.ds(ids_s[i, 0, slot * n_rows + row], 1), :]
+                    row_sum = line if row_sum is None else row_sum + line
+                total[i % 2, pl.ds(row, 1), :] = row_sum
+            sums[chip] = total[i % 2].astype(BF16)
+            if i > 0:
+                send_sums(plane, i - 1).start()
+            if i % batch == batch - 1:
+
+                @pl.when(j < at.side - 1)
+                def _():
+                    fetch(at.plane(j + 1), i - batch + 1, i + 1)
+                    if i == in_plane - 1:
+                        send_sums(plane, i).start()
+
+    repeat(0, at.side, one_plane)
+    got[at.chip] = sums[at.chip]
+
+    repeat(EARLY, n_cand, arrived_group)
+    loads["length"].wait()
+    length = length_s[0]
     live = lax.broadcasted_iota(jnp.int32, scores.shape, 1) < length
     weights = jnp.where(live, scores[...], 0.0).astype(BF16)
     weighted = jnp.dot(weights, history[...], preferred_element_type=F32)
@@ -250,45 +323,40 @@
     weighted = weighted * (1.0 / root)
     interest[...] = weighted.reshape(interest.shape)
 
-    repeat(1, at.chips, lambda step: ids_from(step).wait_recv())
-    to_scalar = pltpu.make_async_copy(ids_got, ids_s, ids_sem)
-    to_scalar.start()
-    for i in range(parts):
-        swap(i).wait_recv()
-        widen(other, 1 - at.core, i * part, part)
     back[at.cand] = interest[at.cand]
+    for name in ("rows", "w_first"):
+        loads[name].wait()
+    table_width = w_first.shape[0] - 3 * width
+    hidden_ref[...] = jnp.dot(
+        target_rows[...], w_first[pl.ds(table_width + width, width), :], preferred_element_type=F32
+    ) + jnp.dot(leaf_vec, w_first[pl.ds(table_width + 2 * width, width), :], preferred_element_type=F32)
+
     repeat(1, n_cand, lambda step: send_back(step).start())
-    to_scalar.wait()
-
-    def one_source(step):
-        src = source(step)
-
-        @pl.when(step >= 3)
-        def _():
-            send_sums(step - 2).start()
-
-        sums[source(step + at.chips - 1)] = total[...].astype(BF16)
-        for row in range(n_rows):
-            row_sum = None
-            for slot in range(bag):
-                line = table[pl.ds(ids_s[src, 0, slot * n_rows + row], 1), :]
-                row_sum = line if row_sum is None else row_sum + line
-            total[pl.ds(row, 1), :] = row_sum
-
-    repeat(0, at.chips, one_source)
-    sums[source(at.chips - 1)] = total[...].astype(BF16)
-    send_sums(at.chips - 2).start()
-    got[at.chip] = sums[at.chip]
+    for name in ("w_second", "w_third", "w_out"):
+        loads[name].wait()
+
+    def add_plane(plane):
+        first = pl.multiple_of(plane * at.chips_x, in_plane)
+        for t in range(in_plane // halves):
+            both = got[first + 2 * t].astype(F32) + got[first + 2 * t + 1].astype(F32)
+            pooled[:, pl.ds(t * emb, emb)] = both.astype(BF16)
+        depth = in_plane // halves * emb
+        rows = pl.ds(pl.multiple_of(lax.div(plane * at.chips_x, halves) * emb, depth), depth)
+        hidden_ref[...] += jnp.dot(pooled[...], w_first[rows, :], preferred_element_type=F32)
+
+    def far_plane(j):
+        plane = at.plane_from(j)
+        for i in range(in_plane):
+            sums_of(at.chip_in(plane, i)).wait_recv()
+        add_plane(plane)
+
+    repeat(0, at.side - 1, far_plane)
+    for i in range(in_plane - 1):
+        sums_of(at.chip_in(at.grp - at.ys[0], i)).wait_recv()
+    add_plane(at.grp - at.ys[0])
     repeat(1, n_cand, lambda step: back_from(step).wait_recv())
     seen = back[...].reshape(n_rows, width).astype(BF16)
     hidden = hidden_ref[...] + jnp.dot(seen, w_first[pl.ds(table_width, width), :], preferred_element_type=F32)
-    send_sums(at.chips - 1).start()
-    for name in ("w_second", "w_third", "w_out"):
-        loads[name].wait()
-    repeat(1, at.chips, lambda step: sums_from(step).wait_recv())
-    for t in range(tables):
-        pooled[:, pl.ds(t * emb, emb)] = (got[2 * t].astype(F32) + got[2 * t + 1].astype(F32)).astype(BF16)
-    hidden += jnp.dot(pooled[...], w_first[pl.ds(0, table_width), :], preferred_element_type=F32)
     one = jnp.maximum(hidden, 0.0).astype(BF16)
     two = jnp.maximum(jnp.dot(one, w_second[...], preferred_element_type=F32), 0.0).astype(BF16)
     three = jnp.maximum(jnp.dot(two, w_third[...], preferred_element_type=F32), 0.0).astype(BF16)
@@ -299,12 +367,12 @@
     placed = jnp.where(row == lane, logit, 0.0).reshape(n_req, per_req, 128)
     out_ref[...] = jnp.sum(placed, axis=1)[:, :per_req]
 
-    repeat(1, at.chips, lambda step: send_ids(step).wait_send())
+    repeat(1, at.chips, lambda step: ids_of(at.chip_after(step)).wait_send())
     repeat(1, n_cand, lambda step: send_target(step).wait_send())
     for i in range(parts):
         swap(i).wait_send()
     repeat(1, n_cand, lambda step: send_back(step).wait_send())
-    repeat(1, at.chips, lambda step: send_sums(step).wait_send())
+    repeat(1, at.chips, lambda step: sums_of(at.chip_after(step)).wait_send())
 
 
 def on_device(
@@ -342,12 +410,12 @@
             held(0), pltpu.SMEM((1,), jnp.int32), held(2), held(3), held(4), pltpu.VMEM((events, width), BF16),
             held(6), pltpu.VMEM((piece_rows, emb), BF16), held(8), held(9), held(10), held(11),
             held(12), held(13), held(14), held(15),
-            pltpu.VMEM((halves, tables, 1, rows * bag), jnp.int32),
+            pltpu.VMEM((tables, halves, 1, rows * bag), jnp.int32),
             pltpu.VMEM((chips, 1, rows * bag), jnp.int32),
-            pltpu.SMEM((chips, 1, rows * bag), jnp.int32),
+            pltpu.SMEM((chips // math.isqrt(n_grp), 1, rows * bag), jnp.int32),
             pltpu.VMEM((piece_rows, emb), BF16),
             pltpu.VMEM((2 * piece_rows + 8, emb), F32),
-            pltpu.VMEM((rows, emb), F32),
+            pltpu.VMEM((2, rows, emb), F32),
             pltpu.VMEM((chips, rows, emb), BF16),
             pltpu.VMEM((chips, rows, emb), BF16),
             pltpu.VMEM((n_cand, per_req, width), BF16),
@@ -355,9 +423,9 @@
             pltpu.VMEM((n_cand, per_req, width), F32),
             pltpu.VMEM((rows, events), F32),
             pltpu.VMEM((per_req * att, width), BF16),
-            pltpu.VMEM((rows, tables * emb), BF16),
+            pltpu.VMEM((rows, tables * emb // math.isqrt(n_grp)), BF16),
             pltpu.VMEM((rows, w_first.shape[1]), F32),
-            dma((len(args),)), dma((chips,)), dma((chips,)), dma(()), dma((PARTS,)), dma((PARTS,)),
+            dma((len(args),)), dma((chips,)), dma((chips,)), dma((chips // math.isqrt(n_grp),)), dma((PARTS,)), dma((PARTS,)),
             dma((n_cand,)), dma((n_cand,)), dma((chips,)), dma((chips,)), dma((n_cand,)), dma((n_cand,)),
         ],
         compiler_params=pltpu.CompilerParams(

time: 52.8 us -> 43.9 us (0.83)
  Pallas kernels: 49.5 us -> 40.6 us
    pallas_call x1, Pallas kernels: 49.5 us -> 40.6 us  [on_device(): pl.pallas_call(functools.partial(kernel, n_grp, n_cand), out_shape=jax.Sh...]
where the time goes in v3:
time: 43.9 us; the launch traced here: 43.8 us
  Pallas kernels  40.6 us (92%)
  local copies, waits for them, and re-layouts  2.5 us (6%)
  between operations  0.66 us (2%)
    pallas_call x1, Pallas kernels, on_device(): pl.pallas_call(functools.partial(kernel, n_grp, n_cand), out_shape=jax.Sh...  40.6 us
    unnamed x1, local copies, waits for them, and re-layouts  1.28 us
    reshape x1, local copies, waits for them, and re-layouts, on_device(): w_out.reshape(1, -1)  1.22 us

profile of v3, /device:TPU:1, one launch (start us, length us, event | category | flops | bytes accessed | tf_op | source)
XLA Modules:
  0.0 43.8 jit_solution(11063313850150414547)
XLA Ops:
  0.7 1.2 %reshape.23.w_out_hbm = bf16[1,256]{1,0:T(2,128)(2,1)} reshape(bf16[256]{0:T(256)(128)(2,1)} %param.29) | data formatting | bytes 1024 | tf_op jit(solution)/shard_map/reshape | solution.py:398
  1.9 40.6 %rank.1 = f32[8,8]{1,0:T(8,128)} custom-call(s32[64,4,32]{2,1,0:T(4,128)} %bitcast.8, s32[1]{0:T(128)S(6)} %copy.17.length_hbm, bf16[8,8,256]{2,1,0:T(8,128)(2,1)} %target_hbm.1, bf16[64,256]{1,0:T(8,128)(2,1)} %bitcast.9, s32[64,64]{1,0:T(8,128)} %bitcast.10, bf16[1,1024,256]{2,1,0:T(8,128)(2,1)} %history_hbm.1, bf16[2048,256]{1,0:T(8,128)(2,1)} %bitcast.7, ...), custom_call_target="tpu_custom_call" | custom-call | tf_op jit(solution)/shard_map/rank/pallas_call | solution.py:404
  42.5 1.3 %copy.18 = f32[8,8]{1,0:T(8,128)} copy(f32[8,8]{1,0:T(8,128)} %rank.1) | data formatting | bytes 512

commit v4 on v3

--- a/solution.py
+++ b/solution.py
@@ -252,13 +252,6 @@
 
     one_group(0)
 
-    pl.semaphore_wait(barrier, count)
-    repeat(1, n_cand, lambda step: send_target(step).start())
-    at.each_other_chip(lambda plane, i: send_ids(plane, i).start())
-    own_ids.start()
-    for i in range(parts):
-        swap(i).start()
-
     for name in ("leaf_ids", "leaf"):
         loads[name].wait()
     trees = leaf_ids.shape[1]
@@ -270,6 +263,20 @@
     leaf_of = lax.broadcasted_iota(jnp.int32, wide.shape, 1) % leaves
     hot = (wide == leaf_of.astype(F32)).astype(F32).astype(BF16)
     leaf_vec = jnp.dot(hot, leaf_table[...], preferred_element_type=F32).astype(BF16)
+    for name in ("rows", "w_first"):
+        loads[name].wait()
+    table_width = w_first.shape[0] - 3 * width
+    hidden_ref[...] = jnp.dot(
+        target_rows[...], w_first[pl.ds(table_width + width, width), :], preferred_element_type=F32
+    ) + jnp.dot(leaf_vec, w_first[pl.ds(table_width + 2 * width, width), :], preferred_element_type=F32)
+
+    pl.semaphore_wait(barrier, count)
+    repeat(1, n_cand, lambda step: send_target(step).start())
+    at.each_other_chip(lambda plane, i: send_ids(plane, i).start())
+    own_ids.start()
+    for i in range(parts):
+        swap(i).start()
+
     repeat(1, EARLY, arrived_group)
 
     def to_scalar(chip, i):
@@ -324,13 +331,6 @@
     interest[...] = weighted.reshape(interest.shape)
 
     back[at.cand] = interest[at.cand]
-    for name in ("rows", "w_first"):
-        loads[name].wait()
-    table_width = w_first.shape[0] - 3 * width
-    hidden_ref[...] = jnp.dot(
-        target_rows[...], w_first[pl.ds(table_width + width, width), :], preferred_element_type=F32
-    ) + jnp.dot(leaf_vec, w_first[pl.ds(table_width + 2 * width, width), :], preferred_element_type=F32)
-
     repeat(1, n_cand, lambda step: send_back(step).start())
     for name in ("w_second", "w_third", "w_out"):
         loads[name].wait()
@@ -360,7 +360,7 @@
     one = jnp.maximum(hidden, 0.0).astype(BF16)
     two = jnp.maximum(jnp.dot(one, w_second[...], preferred_element_type=F32), 0.0).astype(BF16)
     three = jnp.maximum(jnp.dot(two, w_third[...], preferred_element_type=F32), 0.0).astype(BF16)
-    logit = jnp.sum(three.astype(F32) * w_out[...].astype(F32), axis=1, keepdims=True)
+    logit = jnp.sum(three.astype(F32) * w_out[...].astype(F32).reshape(1, -1), axis=1, keepdims=True)
     n_req, per_req = out_ref.shape
     row = lax.broadcasted_iota(jnp.int32, (n_rows, 128), 0) % per_req
     lane = lax.broadcasted_iota(jnp.int32, (n_rows, 128), 1)
@@ -395,7 +395,7 @@
         jnp.transpose(bag_ids, (0, 1, 3, 2)).reshape(rows, bag, tables), lengths, target,
         target.reshape(rows, width), leaf_ids.reshape(rows, trees), history,
         leaf_table.reshape(trees * leaves, width), table_piece, w_query, w_key, w_pair, a_out.reshape(1, att),
-        w_first, w_second, w_third, w_out.reshape(1, -1),
+        w_first, w_second, w_third, w_out,
     )
 
     def held(i):

time: 43.9 us -> 43.9 us (level)
  local copies, waits for them, and re-layouts: 2.5 us -> 1.28 us
  Pallas kernels: 40.6 us -> 41.8 us
    reshape x1 -> x0, local copies, waits for them, and re-layouts: 1.22 us -> none  [on_device(): w_out.reshape(1, -1)]
    pallas_call x1, Pallas kernels: 40.6 us -> 41.8 us  [on_device(): pl.pallas_call(functools.partial(kernel, n_grp, n_cand), out_shape=jax.Sh...]
where the time goes in v4:
time: 43.9 us; the launch traced here: 43.7 us
  Pallas kernels  41.8 us (95%)
  local copies, waits for them, and re-layouts  1.28 us (3%)
  between operations  0.66 us (2%)
    pallas_call x1, Pallas kernels, on_device(): pl.pallas_call(functools.partial(kernel, n_grp, n_cand), out_shape=jax.Sh...  41.8 us
    unnamed x1, local copies, waits for them, and re-layouts  1.28 us

profile of v4, /device:TPU:1, one launch (start us, length us, event | category | flops | bytes accessed | tf_op | source)
XLA Modules:
  0.0 43.7 jit_solution(4378870254096764802)
XLA Ops:
  0.7 41.8 %rank.1 = f32[8,8]{1,0:T(8,128)} custom-call(s32[64,4,32]{2,1,0:T(4,128)} %bitcast.8, s32[1]{0:T(128)S(6)} %copy.17.length_hbm, bf16[8,8,256]{2,1,0:T(8,128)(2,1)} %target_hbm.1, bf16[64,256]{1,0:T(8,128)(2,1)} %bitcast.9, s32[64,64]{1,0:T(8,128)} %bitcast.10, bf16[1,1024,256]{2,1,0:T(8,128)(2,1)} %history_hbm.1, bf16[2048,256]{1,0:T(8,128)(2,1)} %bitcast.7, ...), custom_call_target="tpu_custom_call" | custom-call | tf_op jit(solution)/shard_map/rank/pallas_call | solution.py:404
  42.4 1.3 %copy.18 = f32[8,8]{1,0:T(8,128)} copy(f32[8,8]{1,0:T(8,128)} %rank.1) | data formatting | bytes 512
